TPU v7x, 128 devices: a whole 4x4x4 slice. The times are simulated.
128 devices in a mesh: px: 16 (over y, x), py: 8 (over z, core).
Axes of the slice: x: 4, y: 4, z: 4, core: 2. Of those that a mesh axis runs over, the one named last changes fastest.
Arguments:
- fields: bfloat16 [4, 16, 1024, 1024], P(None, None, 'px', 'py'), may hold values from -6 to 6
- x_operators: bfloat16 [3, 1024, 1024], replicated
- y_operators: bfloat16 [3, 1024, 1024], replicated
- viscosity: float32 [4], replicated, may hold values from 0.1 to 1
- wall_tile: int32 [16384], P(('px', 'py')), may hold values from 0 to 1023
- wall_owner: int32 [16384, 1], P(('px', 'py')), may hold values from 0 to 127; in each aligned block of 128 rows (0 to 127, 128 to 255, ...) at most 4 rows name the same one
- wall_row: int32 [16384], P(('px', 'py')), may hold values from 0 to 63
- solid_temp: float32 [1024, 1024], P('px', 'py'), may hold values from -6 to 6
- conductivity: float32 [1024, 1024], P('px', 'py'), may hold values from 0.2 to 1
Outputs:
- new_fields: bfloat16 [4, 16, 1024, 1024], P(None, None, 'px', 'py')
- new_solid: float32 [1024, 1024], P('px', 'py')
Inputs may be any that keep to these rules, and one draw needn't show every extreme that they name: `wall_owner`: at most 4 of one device's wall slots name the same owner, and some owner receives exactly 4 of them. `wall_tile`: A y-line of the sending device's own block, numbered z times its x cells plus its local x.
All inputs are finite; a program needn't handle non-finite values.
Results may differ from a plain program's by a relative error of at most 0.0054.
Values may be sent and summed in bfloat16 or wider, within the bound.
A program may use at most 64 MiB of HBM per device.

v0:
```python
import jax
import jax.numpy as jnp
from jax import lax
from jax.sharding import PartitionSpec as P

COND_STEPS = 8


time_step = 0.25
wall_gain = 0.5
diffusion_rate = 0.24
source_gain = 0.1


def with_halo(block, sides, width):
    for axis, dim in sides:
        count = lax.axis_size(axis)
        forward = [(i, i + 1) for i in range(count - 1)]
        backward = [(target, source) for source, target in forward]
        low = lax.ppermute(
            lax.slice_in_dim(block, block.shape[dim] - width, None, axis=dim), axis, forward
        )
        high = lax.ppermute(lax.slice_in_dim(block, 0, width, axis=dim), axis, backward)
        block = jnp.concatenate([low, block, high], axis=dim)
    return block


def on_device(
    fields,
    x_operators,
    y_operators,
    viscosity,
    wall_tile,
    wall_owner,
    wall_row,
    solid_temp,
    conductivity,
):
    rates = viscosity[:, None, None, None]
    x_rows = lax.all_to_all(fields, "px", split_axis=1, concat_axis=2, tiled=True)
    result = jnp.einsum("oij,fzjy->ofziy", x_operators, x_rows, preferred_element_type=jnp.float32)
    speed = x_rows[0].astype(jnp.float32)
    half_step = lax.all_to_all(
        (result[2] + time_step * (-speed * result[0] + rates * result[1])).astype(jnp.bfloat16),
        "px",
        split_axis=2,
        concat_axis=1,
        tiled=True,
    )
    y_rows = lax.all_to_all(half_step, "py", split_axis=1, concat_axis=3, tiled=True)
    result = jnp.einsum("oij,fzxj->ofzxi", y_operators, y_rows, preferred_element_type=jnp.float32)
    speed = y_rows[1].astype(jnp.float32)
    new_fields = lax.all_to_all(
        (result[2] + time_step * (-speed * result[0] + rates * result[1])).astype(jnp.bfloat16),
        "py",
        split_axis=3,
        concat_axis=1,
        tiled=True,
    )
    width = new_fields.shape[3]
    theta_lines = new_fields[3].reshape(-1, width)
    flux = wall_gain * jnp.take(theta_lines, wall_tile, axis=0).astype(jnp.float32)
    owner = wall_owner[:, 0]
    across_px = lax.axis_size("px")
    across_py = lax.axis_size("py")
    devices = across_px * across_py
    capacity = max(2, 4 * wall_tile.shape[0] // devices)
    onehot = (owner[:, None] == jnp.arange(devices, dtype=jnp.int32)[None, :]).astype(jnp.int32)
    earlier = jnp.cumsum(onehot, axis=0) - onehot
    position = jnp.sum(earlier * onehot, axis=1)
    sending = jnp.zeros((devices, capacity, width), jnp.float32).at[owner, position].set(flux)
    labels = jnp.full((devices, capacity), -1, jnp.int32).at[owner, position].set(wall_row)
    arrived, tags = (
        lax.all_to_all(
            sending.astype(jnp.bfloat16), ("px", "py"), split_axis=0, concat_axis=0, tiled=True
        ).astype(sending.dtype),
        lax.all_to_all(labels, ("px", "py"), split_axis=0, concat_axis=0, tiled=True),
    )
    solid_rows = solid_temp.shape[0]
    selector = (
        tags.reshape(-1)[None, :] == jnp.arange(solid_rows, dtype=jnp.int32)[:, None]
    ).astype(jnp.float32)
    source = jnp.dot(
        selector,
        arrived.reshape(-1, width),
        precision=lax.Precision.HIGHEST,
        preferred_element_type=jnp.float32,
    )
    margin_max = COND_STEPS
    kappa_ext, source_ext = (
        with_halo(conductivity, (("px", 0), ("py", 1)), margin_max),
        with_halo(source, (("px", 0), ("py", 1)), margin_max),
    )
    row_index = (
        lax.axis_index("px") * solid_rows
        - margin_max
        + jnp.arange(solid_rows + 2 * margin_max, dtype=jnp.int32)
    )
    col_index = (
        lax.axis_index("py") * width
        - margin_max
        + jnp.arange(width + 2 * margin_max, dtype=jnp.int32)
    )
    row_valid = (row_index >= 0) & (row_index < across_px * solid_rows)
    col_valid = (col_index >= 0) & (col_index < across_py * width)
    inside = (row_valid[:, None] & col_valid[None, :]).astype(jnp.float32)
    depth = 1
    temp = solid_temp
    offset = margin_max - depth
    for _ in range(COND_STEPS // depth):
        extended = with_halo(temp, (("px", 0), ("py", 1)), depth)
        rows_end = offset + solid_rows + 2 * depth
        cols_end = offset + width + 2 * depth
        relax_temp = extended
        kappa = kappa_ext[offset:rows_end, offset:cols_end]
        heat = source_ext[offset:rows_end, offset:cols_end]
        keep = inside[offset:rows_end, offset:cols_end]
        centre = relax_temp[1:-1, 1:-1]
        kcentre = kappa[1:-1, 1:-1]
        near = [
            (relax_temp[2:, 1:-1], kappa[2:, 1:-1]),
            (relax_temp[:-2, 1:-1], kappa[:-2, 1:-1]),
            (relax_temp[1:-1, 2:], kappa[1:-1, 2:]),
            (relax_temp[1:-1, :-2], kappa[1:-1, :-2]),
        ]
        laplace = jnp.zeros(centre.shape, jnp.float32)
        for tnear, knear in near:
            laplace = laplace + 0.5 * (kcentre + knear) * (tnear - centre)
        relax_temp = (centre + diffusion_rate * laplace + source_gain * heat[1:-1, 1:-1]) * keep[
            1:-1, 1:-1
        ]
        kappa = kcentre
        heat = heat[1:-1, 1:-1]
        keep = keep[1:-1, 1:-1]
        temp = relax_temp
    return (new_fields, temp)


def solution(mesh):
    return jax.shard_map(
        on_device,
        mesh=mesh,
        in_specs=(
            P(None, None, "px", "py"),
            P(),
            P(),
            P(),
            P(("px", "py")),
            P(("px", "py"), None),
            P(("px", "py")),
            P("px", "py"),
            P("px", "py"),
        ),
        out_specs=(P(None, None, "px", "py"), P("px", "py")),
        check_vma=False,
    )
```

profile of v0, /device:TPU:1, one launch (start us, length us, event | category | flops | bytes accessed | tf_op | source)
XLA Modules:
  0.0 263.5 jit_solution(11270359746205560965)
XLA Ops:
  1.9 23.4 %all_to_all.71 = bf16[4,16,64,128]{3,2,0,1:T(8,128)(2,1)S(1)} all-to-all(bf16[4,16,64,128]{3,2,0,1:T(8,128)(2,1)S(1)} %copy.31), channel_id=1, replica_groups=mesh['px'=16,'py'=8] {'px'}, dimensions={1} | all-to-all | bytes 2097152 | tf_op jit(solution)/shard_map/all_to_all | solution.py:40
  25.7 5.7 %fusion.4 = f32[3,4,1,1024,128]{3,4,0,1,2:T(8,128)S(1)} fusion(bf16[4,1024,128,1]{2,1,3,0:T(8,128)(2,1)S(1)} %bitcast.118, bf16[3,1024,1024]{2,1,0:T(8,128)(2,1)} %param.10), kind=kOutput, calls=%fused_computation.7 | convolution fusion | flops 3221225472 | bytes 13631488 | tf_op jit(solution)/shard_map/oij,fzjy->ofziy/dot_general | solution.py:41
  33.8 3.7 %all-to-all-start.1 = ((bf16[4,1,1024,128]{3,0,1,2:T(4,128)(2,1)}), bf16[4,1,1024,128]{3,0,1,2:T(4,128)(2,1)S(1)}, u32[]{:S(2)}, u32[]{:S(2)}) async-start(bf16[4,1,1024,128]{3,0,1,2:T(4,128)(2,1)} %copy.37), calls=%async_computation.1 | async-start | bytes 2097152 | tf_op jit(solution)/shard_map/all_to_all | solution.py:43
  37.5 3.1 %collective-permute-start.3 = (f32[1,128]{1,0:T(1,128)S(1)}, f32[1,128]{1,0:T(1,128)S(1)}, u32[]{:S(2)}, u32[]{:S(2)}) collective-permute-start(f32[1,128]{1,0:T(1,128)S(1)} %get-tuple-element.39), channel_id=1, source_target_pairs={{0,8},{8,16},{16,24},{24,32},{32,40},{40,48},{48,56},{56,64},{64,7... | collective-permute-start | bytes 1544 | tf_op jit(solution)/shard_map/ppermute | solution.py:20
  41.9 4.0 %collective-permute-start.2 = (f32[8,128]{1,0:T(8,128)S(1)}, f32[8,128]{1,0:T(8,128)S(1)}, u32[]{:S(2)}, u32[]{:S(2)}) collective-permute-start(f32[8,128]{1,0:T(8,128)S(1)} %get-tuple-element.37), channel_id=1, source_target_pairs={{0,8},{8,16},{16,24},{24,32},{32,40},{40,48},{48,56},{56,64},{64,7... | collective-permute-start | bytes 12296 | tf_op jit(solution)/shard_map/ppermute | solution.py:20
  47.2 5.2 %all-to-all-done.1 = bf16[4,1,1024,128]{3,0,1,2:T(4,128)(2,1)S(1)} async-done(((bf16[4,1,1024,128]{3,0,1,2:T(4,128)(2,1)}), bf16[4,1,1024,128]{3,0,1,2:T(4,128)(2,1)S(1)}, u32[]{:S(2)}, u32[]{:S(2)}) %all-to-all-start.1) | async-done | bytes 1048608 | tf_op jit(solution)/shard_map/all_to_all | solution.py:43
  53.7 8.7 %all-to-all-start.2 = ((bf16[4,16,64,128]{3,2,0,1:T(8,128)(2,1)}), bf16[4,16,64,128]{3,2,0,1:T(8,128)(2,1)S(1)}, u32[]{:S(2)}, u32[]{:S(2)}) async-start(bf16[4,16,64,128]{3,2,0,1:T(8,128)(2,1)} %copy.39), calls=%async_computation.2 | async-start | bytes 2097152 | tf_op jit(solution)/shard_map/all_to_all | solution.py:50
  62.9 14.5 %all-to-all-done.2 = bf16[4,16,64,128]{3,2,0,1:T(8,128)(2,1)S(1)} async-done(((bf16[4,16,64,128]{3,2,0,1:T(8,128)(2,1)}), bf16[4,16,64,128]{3,2,0,1:T(8,128)(2,1)S(1)}, u32[]{:S(2)}, u32[]{:S(2)}) %all-to-all-start.2) | async-done | bytes 1048608 | tf_op jit(solution)/shard_map/all_to_all | solution.py:50
  78.7 5.6 %fusion.7 = f32[3,4,2,64,1024]{4,3,0,2,1:T(8,128)S(1)} fusion(bf16[3,1024,1024]{2,1,0:T(8,128)(2,1)} %param.11, bf16[4,2,64,1024,1]{3,2,1,0,4:T(8,128)(2,1)S(1)} %reshape.159), kind=kOutput, calls=%fused_computation.8 | convolution fusion | flops 3221225472 | bytes 13631488 | tf_op jit(solution)/shard_map/oij,fzxj->ofzxi/dot_general | solution.py:51
  87.0 2.7 %reshape.171 = bf16[8,2,32768]{2,1,0:T(2,128)(2,1)} reshape(bf16[1024,4,2,64]{3,2,1,0:T(2,128)(2,1)S(1)} %bitcast.109) | data formatting | bytes 2097152
  89.6 4.4 %all-to-all-start.3 = ((bf16[8,2,32768]{2,1,0:T(2,128)(2,1)}), bf16[8,2,32768]{2,1,0:T(2,128)(2,1)S(1)}, u32[]{:S(2)}, u32[]{:S(2)}) async-start(bf16[8,2,32768]{2,1,0:T(2,128)(2,1)} %reshape.171), calls=%async_computation.3 | async-start | bytes 2097152 | tf_op jit(solution)/shard_map/all_to_all | solution.py:53
  94.2 6.4 %scatter_fusion = s32[128,4]{0,1:T(4,128)S(1)} fusion(s32[128,4]{0,1:T(4,128)S(1)} %broadcast_in_dim.16, s32[128]{0:T(128)S(1)} %fusion.146, s32[128]{0:T(128)S(1)} %copy-done.5), kind=kCustom, calls=%fused_computation.1 | custom fusion | bytes 2560 | tf_op jit(solution)/shard_map/scatter | solution.py:72
  101.4 3.5 %collective-permute-start.6 = (f32[80,8]{1,0:T(8,128)S(1)}, f32[80,8]{1,0:T(8,128)S(1)}, u32[]{:S(2)}, u32[]{:S(2)}) collective-permute-start(f32[80,8]{1,0:T(8,128)S(1)} %get-tuple-element.5), channel_id=1, source_target_pairs={{0,1},{1,2},{2,3},{3,4},{4,5},{5,6},{6,7},{8,9},{9,10},{10,11},{11... | collective-permute-start | bytes 7688 | tf_op jit(solution)/shard_map/ppermute | solution.py:20
  105.0 1.9 collective-permute-start.4
  106.9 2.1 all-to-all-done.3
  109.1 5.4 %all-to-all-start.4 = ((s32[128,1,4]{2,1,0:T(1,128)}), s32[128,1,4]{2,1,0:T(1,128)S(1)}, u32[]{:S(2)}, u32[]{:S(2)}) async-start(s32[128,1,4]{2,1,0:T(1,128)} %copy.45), calls=%async_computation.4 | async-start | bytes 131072 | tf_op jit(solution)/shard_map/all_to_all | solution.py:77
  116.0 2.6 copy.44
  119.7 6.6 %scatter_fusion.1 = f32[128,4,128]{2,1,0:T(4,128)S(1)} fusion(f32[128,4,128]{2,1,0:T(4,128)S(1)} %broadcast_in_dim.17, s32[128]{0:T(128)S(1)} %fusion.146, f32[128,128]{1,0:T(8,128)S(1)} %convert_multiply_fusion), kind=kCustom, calls=%fused_computation.2 | custom fusion | bytes 197632 | tf_op jit(solution)/shard_map/scatter | solution.py:71
  127.0 9.8 %all-to-all-start.5 = ((bf16[128,4,128]{2,1,0:T(4,128)(2,1)}), bf16[128,4,128]{2,1,0:T(4,128)(2,1)S(1)}, u32[]{:S(2)}, u32[]{:S(2)}) async-start(bf16[128,4,128]{2,1,0:T(4,128)(2,1)} %convert_element_type.50), calls=%async_computation.5 | async-start | bytes 262144 | tf_op jit(solution)/shard_map/all_to_all | solution.py:74
  136.8 3.0 %collective-permute-start.5 = (f32[66,1]{1,0:T(8,128)S(1)}, f32[66,1]{1,0:T(8,128)S(1)}, u32[]{:S(2)}, u32[]{:S(2)}) collective-permute-start(f32[66,1]{1,0:T(8,128)S(1)} %get-tuple-element.21), channel_id=1, source_target_pairs={{1,0},{2,1},{3,2},{4,3},{5,4},{6,5},{7,6},{9,8},{10,9},{11,10},{12... | collective-permute-start | bytes 800 | tf_op jit(solution)/shard_map/ppermute | solution.py:23
  139.8 2.6 collective-permute-start.7
  144.0 2.6 all-to-all-done.5
  147.5 2.2 collective-permute-start.9
  151.0 3.0 %collective-permute-done.8 = f32[1,128]{1,0:T(1,128)S(1)} collective-permute-done((f32[1,128]{1,0:T(1,128)S(1)}, f32[1,128]{1,0:T(1,128)S(1)}, u32[]{:S(2)}, u32[]{:S(2)}) %collective-permute-start.8) | collective-permute-done | bytes 544 | tf_op jit(solution)/shard_map/ppermute | solution.py:23
  154.1 4.2 %collective-permute-start.10 = (f32[66,1]{1,0:T(8,128)S(1)}, f32[66,1]{1,0:T(8,128)S(1)}, u32[]{:S(2)}, u32[]{:S(2)}) collective-permute-start(f32[66,1]{1,0:T(8,128)S(1)} %get-tuple-element.19), channel_id=1, source_target_pairs={{1,0},{2,1},{3,2},{4,3},{5,4},{6,5},{7,6},{9,8},{10,9},{11,10},{12... | collective-permute-start | bytes 800 | tf_op jit(solution)/shard_map/ppermute | solution.py:23
  158.3 1.9 collective-permute-start.11
  161.5 2.4 collective-permute-start.13
  165.2 3.0 %collective-permute-done.12 = f32[1,128]{1,0:T(1,128)S(1)} collective-permute-done((f32[1,128]{1,0:T(1,128)S(1)}, f32[1,128]{1,0:T(1,128)S(1)}, u32[]{:S(2)}, u32[]{:S(2)}) %collective-permute-start.12) | collective-permute-done | bytes 544 | tf_op jit(solution)/shard_map/ppermute | solution.py:23
  168.3 3.2 %collective-permute-start.14 = (f32[66,1]{1,0:T(8,128)S(1)}, f32[66,1]{1,0:T(8,128)S(1)}, u32[]{:S(2)}, u32[]{:S(2)}) collective-permute-start(f32[66,1]{1,0:T(8,128)S(1)} %get-tuple-element.17), channel_id=1, source_target_pairs={{1,0},{2,1},{3,2},{4,3},{5,4},{6,5},{7,6},{9,8},{10,9},{11,10},{12... | collective-permute-start | bytes 800 | tf_op jit(solution)/shard_map/ppermute | solution.py:23
  171.5 4.4 %collective-permute-start.15 = (f32[66,1]{1,0:T(8,128)S(1)}, f32[66,1]{1,0:T(8,128)S(1)}, u32[]{:S(2)}, u32[]{:S(2)}) collective-permute-start(f32[66,1]{1,0:T(8,128)S(1)} %get-tuple-element.18), channel_id=1, source_target_pairs={{0,1},{1,2},{2,3},{3,4},{4,5},{5,6},{6,7},{8,9},{9,10},{10,11},{11... | collective-permute-start | bytes 800 | tf_op jit(solution)/shard_map/ppermute | solution.py:20
  177.1 5.0 %collective-permute-start.17 = (f32[1,128]{1,0:T(1,128)S(1)}, f32[1,128]{1,0:T(1,128)S(1)}, u32[]{:S(2)}, u32[]{:S(2)}) collective-permute-start(f32[1,128]{1,0:T(1,128)S(1)} %get-tuple-element.31), channel_id=1, source_target_pairs={{0,8},{8,16},{16,24},{24,32},{32,40},{40,48},{48,56},{56,64},{64,7... | collective-permute-start | bytes 1544 | tf_op jit(solution)/shard_map/ppermute | solution.py:20
  183.4 3.3 %collective-permute-done.16 = f32[1,128]{1,0:T(1,128)S(1)} collective-permute-done((f32[1,128]{1,0:T(1,128)S(1)}, f32[1,128]{1,0:T(1,128)S(1)}, u32[]{:S(2)}, u32[]{:S(2)}) %collective-permute-start.16) | collective-permute-done | bytes 544 | tf_op jit(solution)/shard_map/ppermute | solution.py:23
  186.8 1.9 collective-permute-start.18
  188.7 5.4 %collective-permute-start.19 = (f32[66,1]{1,0:T(8,128)S(1)}, f32[66,1]{1,0:T(8,128)S(1)}, u32[]{:S(2)}, u32[]{:S(2)}) collective-permute-start(f32[66,1]{1,0:T(8,128)S(1)} %get-tuple-element.16), channel_id=1, source_target_pairs={{0,1},{1,2},{2,3},{3,4},{4,5},{5,6},{6,7},{8,9},{9,10},{10,11},{11... | collective-permute-start | bytes 800 | tf_op jit(solution)/shard_map/ppermute | solution.py:20
  195.2 3.7 %collective-permute-start.21 = (f32[1,128]{1,0:T(1,128)S(1)}, f32[1,128]{1,0:T(1,128)S(1)}, u32[]{:S(2)}, u32[]{:S(2)}) collective-permute-start(f32[1,128]{1,0:T(1,128)S(1)} %get-tuple-element.29), channel_id=1, source_target_pairs={{0,8},{8,16},{16,24},{24,32},{32,40},{40,48},{48,56},{56,64},{64,7... | collective-permute-start | bytes 1544 | tf_op jit(solution)/shard_map/ppermute | solution.py:20
  200.3 3.3 %collective-permute-done.20 = f32[1,128]{1,0:T(1,128)S(1)} collective-permute-done((f32[1,128]{1,0:T(1,128)S(1)}, f32[1,128]{1,0:T(1,128)S(1)}, u32[]{:S(2)}, u32[]{:S(2)}) %collective-permute-start.20) | collective-permute-done | bytes 544 | tf_op jit(solution)/shard_map/ppermute | solution.py:23
  203.7 1.9 collective-permute-start.22
  205.6 5.4 %collective-permute-start.23 = (f32[66,1]{1,0:T(8,128)S(1)}, f32[66,1]{1,0:T(8,128)S(1)}, u32[]{:S(2)}, u32[]{:S(2)}) collective-permute-start(f32[66,1]{1,0:T(8,128)S(1)} %get-tuple-element.14), channel_id=1, source_target_pairs={{0,1},{1,2},{2,3},{3,4},{4,5},{5,6},{6,7},{8,9},{9,10},{10,11},{11... | collective-permute-start | bytes 800 | tf_op jit(solution)/shard_map/ppermute | solution.py:20
  212.1 3.7 %collective-permute-start.25 = (f32[1,128]{1,0:T(1,128)S(1)}, f32[1,128]{1,0:T(1,128)S(1)}, u32[]{:S(2)}, u32[]{:S(2)}) collective-permute-start(f32[1,128]{1,0:T(1,128)S(1)} %get-tuple-element.27), channel_id=1, source_target_pairs={{0,8},{8,16},{16,24},{24,32},{32,40},{40,48},{48,56},{56,64},{64,7... | collective-permute-start | bytes 1544 | tf_op jit(solution)/shard_map/ppermute | solution.py:20
  217.2 3.3 %collective-permute-done.24 = f32[1,128]{1,0:T(1,128)S(1)} collective-permute-done((f32[1,128]{1,0:T(1,128)S(1)}, f32[1,128]{1,0:T(1,128)S(1)}, u32[]{:S(2)}, u32[]{:S(2)}) %collective-permute-start.24) | collective-permute-done | bytes 544 | tf_op jit(solution)/shard_map/ppermute | solution.py:23
  220.6 1.9 collective-permute-start.26
  222.5 5.4 %collective-permute-start.27 = (f32[66,1]{1,0:T(8,128)S(1)}, f32[66,1]{1,0:T(8,128)S(1)}, u32[]{:S(2)}, u32[]{:S(2)}) collective-permute-start(f32[66,1]{1,0:T(8,128)S(1)} %get-tuple-element.12), channel_id=1, source_target_pairs={{0,1},{1,2},{2,3},{3,4},{4,5},{5,6},{6,7},{8,9},{9,10},{10,11},{11... | collective-permute-start | bytes 800 | tf_op jit(solution)/shard_map/ppermute | solution.py:20
  229.1 3.7 %collective-permute-start.29 = (f32[1,128]{1,0:T(1,128)S(1)}, f32[1,128]{1,0:T(1,128)S(1)}, u32[]{:S(2)}, u32[]{:S(2)}) collective-permute-start(f32[1,128]{1,0:T(1,128)S(1)} %get-tuple-element.25), channel_id=1, source_target_pairs={{0,8},{8,16},{16,24},{24,32},{32,40},{40,48},{48,56},{56,64},{64,7... | collective-permute-start | bytes 1544 | tf_op jit(solution)/shard_map/ppermute | solution.py:20
  234.1 3.3 %collective-permute-done.28 = f32[1,128]{1,0:T(1,128)S(1)} collective-permute-done((f32[1,128]{1,0:T(1,128)S(1)}, f32[1,128]{1,0:T(1,128)S(1)}, u32[]{:S(2)}, u32[]{:S(2)}) %collective-permute-start.28) | collective-permute-done | bytes 544 | tf_op jit(solution)/shard_map/ppermute | solution.py:23
  239.4 5.4 %collective-permute-start.31 = (f32[66,1]{1,0:T(8,128)S(1)}, f32[66,1]{1,0:T(8,128)S(1)}, u32[]{:S(2)}, u32[]{:S(2)}) collective-permute-start(f32[66,1]{1,0:T(8,128)S(1)} %get-tuple-element.10), channel_id=1, source_target_pairs={{0,1},{1,2},{2,3},{3,4},{4,5},{5,6},{6,7},{8,9},{9,10},{10,11},{11... | collective-permute-start | bytes 800 | tf_op jit(solution)/shard_map/ppermute | solution.py:20
  246.0 3.7 %collective-permute-start.33 = (f32[1,128]{1,0:T(1,128)S(1)}, f32[1,128]{1,0:T(1,128)S(1)}, u32[]{:S(2)}, u32[]{:S(2)}) collective-permute-start(f32[1,128]{1,0:T(1,128)S(1)} %get-tuple-element.23), channel_id=1, source_target_pairs={{0,8},{8,16},{16,24},{24,32},{32,40},{40,48},{48,56},{56,64},{64,7... | collective-permute-start | bytes 1544 | tf_op jit(solution)/shard_map/ppermute | solution.py:20
  251.0 3.3 %collective-permute-done.32 = f32[1,128]{1,0:T(1,128)S(1)} collective-permute-done((f32[1,128]{1,0:T(1,128)S(1)}, f32[1,128]{1,0:T(1,128)S(1)}, u32[]{:S(2)}, u32[]{:S(2)}) %collective-permute-start.32) | collective-permute-done | bytes 544 | tf_op jit(solution)/shard_map/ppermute | solution.py:23
  256.3 5.4 %collective-permute-start.35 = (f32[66,1]{1,0:T(8,128)S(1)}, f32[66,1]{1,0:T(8,128)S(1)}, u32[]{:S(2)}, u32[]{:S(2)}) collective-permute-start(f32[66,1]{1,0:T(8,128)S(1)} %get-tuple-element.8), channel_id=1, source_target_pairs={{0,1},{1,2},{2,3},{3,4},{4,5},{5,6},{6,7},{8,9},{9,10},{10,11},{11... | collective-permute-start | bytes 800 | tf_op jit(solution)/shard_map/ppermute | solution.py:20
  (127 shorter events, 41.1 us)
Async XLA Ops:
  25.7 5.7 %copy-start.4 = (f32[4]{0:T(128)S(1)}, f32[4]{0:T(128)}, u32[]{:S(2)}) copy-start(f32[4]{0:T(128)} %param.12) | copy-start | bytes 52
  32.3 5.1 %copy-start.2 = (f32[64,128]{1,0:T(8,128)S(1)}, f32[64,128]{1,0:T(8,128)}, u32[]{:S(2)}) copy-start(f32[64,128]{1,0:T(8,128)} %param.16) | copy-start | bytes 98308
  32.3 9.6 %copy-start = (f32[64,128]{1,0:T(8,128)S(1)}, f32[64,128]{1,0:T(8,128)}, u32[]{:S(2)}) copy-start(f32[64,128]{1,0:T(8,128)} %param.17) | copy-start | bytes 98308
  33.8 18.7 %all-to-all-start.1 = ((bf16[4,1,1024,128]{3,0,1,2:T(4,128)(2,1)}), bf16[4,1,1024,128]{3,0,1,2:T(4,128)(2,1)S(1)}, u32[]{:S(2)}, u32[]{:S(2)}) async-start(bf16[4,1,1024,128]{3,0,1,2:T(4,128)(2,1)} %copy.37), calls=%async_computation.1 | async-start | bytes 2097152 | tf_op jit(solution)/shard_map/all_to_all | solution.py:43
  37.5 63.8 %collective-permute-start.3 = (f32[1,128]{1,0:T(1,128)S(1)}, f32[1,128]{1,0:T(1,128)S(1)}, u32[]{:S(2)}, u32[]{:S(2)}) collective-permute-start(f32[1,128]{1,0:T(1,128)S(1)} %get-tuple-element.39), channel_id=1, source_target_pairs={{0,8},{8,16},{16,24},{24,32},{32,40},{40,48},{48,56},{56,64},{64,7... | collective-permute-start | bytes 1544 | tf_op jit(solution)/shard_map/ppermute | solution.py:20
  40.6 60.7 %collective-permute-start.1 = (f32[1,128]{1,0:T(1,128)S(1)}, f32[1,128]{1,0:T(1,128)S(1)}, u32[]{:S(2)}, u32[]{:S(2)}) collective-permute-start(f32[1,128]{1,0:T(1,128)S(1)} %get-tuple-element.40), channel_id=1, source_target_pairs={{8,0},{16,8},{24,16},{32,24},{40,32},{48,40},{56,48},{64,56},{72,6... | collective-permute-start | bytes 1544 | tf_op jit(solution)/shard_map/ppermute | solution.py:23
  41.9 59.4 %collective-permute-start.2 = (f32[8,128]{1,0:T(8,128)S(1)}, f32[8,128]{1,0:T(8,128)S(1)}, u32[]{:S(2)}, u32[]{:S(2)}) collective-permute-start(f32[8,128]{1,0:T(8,128)S(1)} %get-tuple-element.37), channel_id=1, source_target_pairs={{0,8},{8,16},{16,24},{24,32},{32,40},{40,48},{48,56},{56,64},{64,7... | collective-permute-start | bytes 12296 | tf_op jit(solution)/shard_map/ppermute | solution.py:20
  45.9 55.4 %collective-permute-start = (f32[8,128]{1,0:T(8,128)S(1)}, f32[8,128]{1,0:T(8,128)S(1)}, u32[]{:S(2)}, u32[]{:S(2)}) collective-permute-start(f32[8,128]{1,0:T(8,128)S(1)} %get-tuple-element.38), channel_id=1, source_target_pairs={{8,0},{16,8},{24,16},{32,24},{40,32},{48,40},{56,48},{64,56},{72,6... | collective-permute-start | bytes 12296 | tf_op jit(solution)/shard_map/ppermute | solution.py:23
  52.5 10.0 %copy-start.3 = (s32[128,1]{0,1:T(1,128)S(1)}, s32[128,1]{0,1:T(1,128)}, u32[]{:S(2)}) copy-start(s32[128,1]{0,1:T(1,128)} %param.14) | copy-start | bytes 1540
  52.5 10.4 %copy-start.6 = (s32[128]{0:T(128)S(1)}, s32[128]{0:T(128)}, u32[]{:S(2)}) copy-start(s32[128]{0:T(128)} %param.13) | copy-start | bytes 1540
  53.7 23.7 %all-to-all-start.2 = ((bf16[4,16,64,128]{3,2,0,1:T(8,128)(2,1)}), bf16[4,16,64,128]{3,2,0,1:T(8,128)(2,1)S(1)}, u32[]{:S(2)}, u32[]{:S(2)}) async-start(bf16[4,16,64,128]{3,2,0,1:T(8,128)(2,1)} %copy.39), calls=%async_computation.2 | async-start | bytes 2097152 | tf_op jit(solution)/shard_map/all_to_all | solution.py:50
  87.0 7.2 %copy-start.5 = (s32[128]{0:T(128)S(1)}, s32[128]{0:T(128)}, u32[]{:S(2)}) copy-start(s32[128]{0:T(128)} %param.15) | copy-start | bytes 1540
  89.6 19.4 %all-to-all-start.3 = ((bf16[8,2,32768]{2,1,0:T(2,128)(2,1)}), bf16[8,2,32768]{2,1,0:T(2,128)(2,1)S(1)}, u32[]{:S(2)}, u32[]{:S(2)}) async-start(bf16[8,2,32768]{2,1,0:T(2,128)(2,1)} %reshape.171), calls=%async_computation.3 | async-start | bytes 2097152 | tf_op jit(solution)/shard_map/all_to_all | solution.py:53
  101.4 42.5 %collective-permute-start.6 = (f32[80,8]{1,0:T(8,128)S(1)}, f32[80,8]{1,0:T(8,128)S(1)}, u32[]{:S(2)}, u32[]{:S(2)}) collective-permute-start(f32[80,8]{1,0:T(8,128)S(1)} %get-tuple-element.5), channel_id=1, source_target_pairs={{0,1},{1,2},{2,3},{3,4},{4,5},{5,6},{6,7},{8,9},{9,10},{10,11},{11... | collective-permute-start | bytes 7688 | tf_op jit(solution)/shard_map/ppermute | solution.py:20
  105.0 39.0 %collective-permute-start.4 = (f32[80,8]{1,0:T(8,128)S(1)}, f32[80,8]{1,0:T(8,128)}, u32[]{:S(2)}, u32[]{:S(2)}) collective-permute-start(f32[80,8]{1,0:T(8,128)S(1)} %get-tuple-element.6), channel_id=1, source_target_pairs={{1,0},{2,1},{3,2},{4,3},{5,4},{6,5},{7,6},{9,8},{10,9},{11,10},{12... | collective-permute-start | bytes 7688 | tf_op jit(solution)/shard_map/ppermute | solution.py:23
  109.1 17.9 %all-to-all-start.4 = ((s32[128,1,4]{2,1,0:T(1,128)}), s32[128,1,4]{2,1,0:T(1,128)S(1)}, u32[]{:S(2)}, u32[]{:S(2)}) async-start(s32[128,1,4]{2,1,0:T(1,128)} %copy.45), calls=%async_computation.4 | async-start | bytes 131072 | tf_op jit(solution)/shard_map/all_to_all | solution.py:77
  118.6 1.0 copy-start.1
  127.0 19.6 %all-to-all-start.5 = ((bf16[128,4,128]{2,1,0:T(4,128)(2,1)}), bf16[128,4,128]{2,1,0:T(4,128)(2,1)S(1)}, u32[]{:S(2)}, u32[]{:S(2)}) async-start(bf16[128,4,128]{2,1,0:T(4,128)(2,1)} %convert_element_type.50), calls=%async_computation.5 | async-start | bytes 262144 | tf_op jit(solution)/shard_map/all_to_all | solution.py:74
  136.8 7.1 %collective-permute-start.5 = (f32[66,1]{1,0:T(8,128)S(1)}, f32[66,1]{1,0:T(8,128)S(1)}, u32[]{:S(2)}, u32[]{:S(2)}) collective-permute-start(f32[66,1]{1,0:T(8,128)S(1)} %get-tuple-element.21), channel_id=1, source_target_pairs={{1,0},{2,1},{3,2},{4,3},{5,4},{6,5},{7,6},{9,8},{10,9},{11,10},{12... | collective-permute-start | bytes 800 | tf_op jit(solution)/shard_map/ppermute | solution.py:23
  139.8 4.1 %collective-permute-start.7 = (f32[66,1]{1,0:T(8,128)S(1)}, f32[66,1]{1,0:T(8,128)S(1)}, u32[]{:S(2)}, u32[]{:S(2)}) collective-permute-start(f32[66,1]{1,0:T(8,128)S(1)} %get-tuple-element.22), channel_id=1, source_target_pairs={{0,1},{1,2},{2,3},{3,4},{4,5},{5,6},{6,7},{8,9},{9,10},{10,11},{11... | collective-permute-start | bytes 800 | tf_op jit(solution)/shard_map/ppermute | solution.py:20
  147.5 3.5 %collective-permute-start.9 = (f32[1,128]{1,0:T(1,128)S(1)}, f32[1,128]{1,0:T(1,128)S(1)}, u32[]{:S(2)}, u32[]{:S(2)}) collective-permute-start(f32[1,128]{1,0:T(1,128)S(1)} %get-tuple-element.35), channel_id=1, source_target_pairs={{0,8},{8,16},{16,24},{24,32},{32,40},{40,48},{48,56},{56,64},{64,7... | collective-permute-start | bytes 1544 | tf_op jit(solution)/shard_map/ppermute | solution.py:20
  149.7 4.3 %collective-permute-start.8 = (f32[1,128]{1,0:T(1,128)S(1)}, f32[1,128]{1,0:T(1,128)S(1)}, u32[]{:S(2)}, u32[]{:S(2)}) collective-permute-start(f32[1,128]{1,0:T(1,128)S(1)} %get-tuple-element.36), channel_id=1, source_target_pairs={{8,0},{16,8},{24,16},{32,24},{40,32},{48,40},{56,48},{64,56},{72,6... | collective-permute-start | bytes 1544 | tf_op jit(solution)/shard_map/ppermute | solution.py:23
  154.1 6.2 %collective-permute-start.10 = (f32[66,1]{1,0:T(8,128)S(1)}, f32[66,1]{1,0:T(8,128)S(1)}, u32[]{:S(2)}, u32[]{:S(2)}) collective-permute-start(f32[66,1]{1,0:T(8,128)S(1)} %get-tuple-element.19), channel_id=1, source_target_pairs={{1,0},{2,1},{3,2},{4,3},{5,4},{6,5},{7,6},{9,8},{10,9},{11,10},{12... | collective-permute-start | bytes 800 | tf_op jit(solution)/shard_map/ppermute | solution.py:23
  158.3 3.1 %collective-permute-start.11 = (f32[66,1]{1,0:T(8,128)S(1)}, f32[66,1]{1,0:T(8,128)S(1)}, u32[]{:S(2)}, u32[]{:S(2)}) collective-permute-start(f32[66,1]{1,0:T(8,128)S(1)} %get-tuple-element.20), channel_id=1, source_target_pairs={{0,1},{1,2},{2,3},{3,4},{4,5},{5,6},{6,7},{8,9},{9,10},{10,11},{11... | collective-permute-start | bytes 800 | tf_op jit(solution)/shard_map/ppermute | solution.py:20
  161.5 3.7 %collective-permute-start.13 = (f32[1,128]{1,0:T(1,128)S(1)}, f32[1,128]{1,0:T(1,128)S(1)}, u32[]{:S(2)}, u32[]{:S(2)}) collective-permute-start(f32[1,128]{1,0:T(1,128)S(1)} %get-tuple-element.33), channel_id=1, source_target_pairs={{0,8},{8,16},{16,24},{24,32},{32,40},{40,48},{48,56},{56,64},{64,7... | collective-permute-start | bytes 1544 | tf_op jit(solution)/shard_map/ppermute | solution.py:20
  163.9 4.3 %collective-permute-start.12 = (f32[1,128]{1,0:T(1,128)S(1)}, f32[1,128]{1,0:T(1,128)S(1)}, u32[]{:S(2)}, u32[]{:S(2)}) collective-permute-start(f32[1,128]{1,0:T(1,128)S(1)} %get-tuple-element.34), channel_id=1, source_target_pairs={{8,0},{16,8},{24,16},{32,24},{40,32},{48,40},{56,48},{64,56},{72,6... | collective-permute-start | bytes 1544 | tf_op jit(solution)/shard_map/ppermute | solution.py:23
  168.3 7.6 %collective-permute-start.14 = (f32[66,1]{1,0:T(8,128)S(1)}, f32[66,1]{1,0:T(8,128)S(1)}, u32[]{:S(2)}, u32[]{:S(2)}) collective-permute-start(f32[66,1]{1,0:T(8,128)S(1)} %get-tuple-element.17), channel_id=1, source_target_pairs={{1,0},{2,1},{3,2},{4,3},{5,4},{6,5},{7,6},{9,8},{10,9},{11,10},{12... | collective-permute-start | bytes 800 | tf_op jit(solution)/shard_map/ppermute | solution.py:23
  171.5 5.4 %collective-permute-start.15 = (f32[66,1]{1,0:T(8,128)S(1)}, f32[66,1]{1,0:T(8,128)S(1)}, u32[]{:S(2)}, u32[]{:S(2)}) collective-permute-start(f32[66,1]{1,0:T(8,128)S(1)} %get-tuple-element.18), channel_id=1, source_target_pairs={{0,1},{1,2},{2,3},{3,4},{4,5},{5,6},{6,7},{8,9},{9,10},{10,11},{11... | collective-permute-start | bytes 800 | tf_op jit(solution)/shard_map/ppermute | solution.py:20
  177.1 6.3 %collective-permute-start.17 = (f32[1,128]{1,0:T(1,128)S(1)}, f32[1,128]{1,0:T(1,128)S(1)}, u32[]{:S(2)}, u32[]{:S(2)}) collective-permute-start(f32[1,128]{1,0:T(1,128)S(1)} %get-tuple-element.31), channel_id=1, source_target_pairs={{0,8},{8,16},{16,24},{24,32},{32,40},{40,48},{48,56},{56,64},{64,7... | collective-permute-start | bytes 1544 | tf_op jit(solution)/shard_map/ppermute | solution.py:20
  182.1 4.6 %collective-permute-start.16 = (f32[1,128]{1,0:T(1,128)S(1)}, f32[1,128]{1,0:T(1,128)S(1)}, u32[]{:S(2)}, u32[]{:S(2)}) collective-permute-start(f32[1,128]{1,0:T(1,128)S(1)} %get-tuple-element.32), channel_id=1, source_target_pairs={{8,0},{16,8},{24,16},{32,24},{40,32},{48,40},{56,48},{64,56},{72,6... | collective-permute-start | bytes 1544 | tf_op jit(solution)/shard_map/ppermute | solution.py:23
  186.8 7.3 %collective-permute-start.18 = (f32[66,1]{1,0:T(8,128)S(1)}, f32[66,1]{1,0:T(8,128)S(1)}, u32[]{:S(2)}, u32[]{:S(2)}) collective-permute-start(f32[66,1]{1,0:T(8,128)S(1)} %get-tuple-element.15), channel_id=1, source_target_pairs={{1,0},{2,1},{3,2},{4,3},{5,4},{6,5},{7,6},{9,8},{10,9},{11,10},{12... | collective-permute-start | bytes 800 | tf_op jit(solution)/shard_map/ppermute | solution.py:23
  188.7 6.4 %collective-permute-start.19 = (f32[66,1]{1,0:T(8,128)S(1)}, f32[66,1]{1,0:T(8,128)S(1)}, u32[]{:S(2)}, u32[]{:S(2)}) collective-permute-start(f32[66,1]{1,0:T(8,128)S(1)} %get-tuple-element.16), channel_id=1, source_target_pairs={{0,1},{1,2},{2,3},{3,4},{4,5},{5,6},{6,7},{8,9},{9,10},{10,11},{11... | collective-permute-start | bytes 800 | tf_op jit(solution)/shard_map/ppermute | solution.py:20
  195.2 5.1 %collective-permute-start.21 = (f32[1,128]{1,0:T(1,128)S(1)}, f32[1,128]{1,0:T(1,128)S(1)}, u32[]{:S(2)}, u32[]{:S(2)}) collective-permute-start(f32[1,128]{1,0:T(1,128)S(1)} %get-tuple-element.29), channel_id=1, source_target_pairs={{0,8},{8,16},{16,24},{24,32},{32,40},{40,48},{48,56},{56,64},{64,7... | collective-permute-start | bytes 1544 | tf_op jit(solution)/shard_map/ppermute | solution.py:20
  199.0 4.6 %collective-permute-start.20 = (f32[1,128]{1,0:T(1,128)S(1)}, f32[1,128]{1,0:T(1,128)S(1)}, u32[]{:S(2)}, u32[]{:S(2)}) collective-permute-start(f32[1,128]{1,0:T(1,128)S(1)} %get-tuple-element.30), channel_id=1, source_target_pairs={{8,0},{16,8},{24,16},{32,24},{40,32},{48,40},{56,48},{64,56},{72,6... | collective-permute-start | bytes 1544 | tf_op jit(solution)/shard_map/ppermute | solution.py:23
  203.7 7.3 %collective-permute-start.22 = (f32[66,1]{1,0:T(8,128)S(1)}, f32[66,1]{1,0:T(8,128)S(1)}, u32[]{:S(2)}, u32[]{:S(2)}) collective-permute-start(f32[66,1]{1,0:T(8,128)S(1)} %get-tuple-element.13), channel_id=1, source_target_pairs={{1,0},{2,1},{3,2},{4,3},{5,4},{6,5},{7,6},{9,8},{10,9},{11,10},{12... | collective-permute-start | bytes 800 | tf_op jit(solution)/shard_map/ppermute | solution.py:23
  205.6 6.4 %collective-permute-start.23 = (f32[66,1]{1,0:T(8,128)S(1)}, f32[66,1]{1,0:T(8,128)S(1)}, u32[]{:S(2)}, u32[]{:S(2)}) collective-permute-start(f32[66,1]{1,0:T(8,128)S(1)} %get-tuple-element.14), channel_id=1, source_target_pairs={{0,1},{1,2},{2,3},{3,4},{4,5},{5,6},{6,7},{8,9},{9,10},{10,11},{11... | collective-permute-start | bytes 800 | tf_op jit(solution)/shard_map/ppermute | solution.py:20
  212.1 5.1 %collective-permute-start.25 = (f32[1,128]{1,0:T(1,128)S(1)}, f32[1,128]{1,0:T(1,128)S(1)}, u32[]{:S(2)}, u32[]{:S(2)}) collective-permute-start(f32[1,128]{1,0:T(1,128)S(1)} %get-tuple-element.27), channel_id=1, source_target_pairs={{0,8},{8,16},{16,24},{24,32},{32,40},{40,48},{48,56},{56,64},{64,7... | collective-permute-start | bytes 1544 | tf_op jit(solution)/shard_map/ppermute | solution.py:20
  215.9 4.6 %collective-permute-start.24 = (f32[1,128]{1,0:T(1,128)S(1)}, f32[1,128]{1,0:T(1,128)S(1)}, u32[]{:S(2)}, u32[]{:S(2)}) collective-permute-start(f32[1,128]{1,0:T(1,128)S(1)} %get-tuple-element.28), channel_id=1, source_target_pairs={{8,0},{16,8},{24,16},{32,24},{40,32},{48,40},{56,48},{64,56},{72,6... | collective-permute-start | bytes 1544 | tf_op jit(solution)/shard_map/ppermute | solution.py:23
  220.6 7.3 %collective-permute-start.26 = (f32[66,1]{1,0:T(8,128)S(1)}, f32[66,1]{1,0:T(8,128)S(1)}, u32[]{:S(2)}, u32[]{:S(2)}) collective-permute-start(f32[66,1]{1,0:T(8,128)S(1)} %get-tuple-element.11), channel_id=1, source_target_pairs={{1,0},{2,1},{3,2},{4,3},{5,4},{6,5},{7,6},{9,8},{10,9},{11,10},{12... | collective-permute-start | bytes 800 | tf_op jit(solution)/shard_map/ppermute | solution.py:23
  222.5 6.4 %collective-permute-start.27 = (f32[66,1]{1,0:T(8,128)S(1)}, f32[66,1]{1,0:T(8,128)S(1)}, u32[]{:S(2)}, u32[]{:S(2)}) collective-permute-start(f32[66,1]{1,0:T(8,128)S(1)} %get-tuple-element.12), channel_id=1, source_target_pairs={{0,1},{1,2},{2,3},{3,4},{4,5},{5,6},{6,7},{8,9},{9,10},{10,11},{11... | collective-permute-start | bytes 800 | tf_op jit(solution)/shard_map/ppermute | solution.py:20
  229.1 5.1 %collective-permute-start.29 = (f32[1,128]{1,0:T(1,128)S(1)}, f32[1,128]{1,0:T(1,128)S(1)}, u32[]{:S(2)}, u32[]{:S(2)}) collective-permute-start(f32[1,128]{1,0:T(1,128)S(1)} %get-tuple-element.25), channel_id=1, source_target_pairs={{0,8},{8,16},{16,24},{24,32},{32,40},{40,48},{48,56},{56,64},{64,7... | collective-permute-start | bytes 1544 | tf_op jit(solution)/shard_map/ppermute | solution.py:20
  232.8 4.6 %collective-permute-start.28 = (f32[1,128]{1,0:T(1,128)S(1)}, f32[1,128]{1,0:T(1,128)S(1)}, u32[]{:S(2)}, u32[]{:S(2)}) collective-permute-start(f32[1,128]{1,0:T(1,128)S(1)} %get-tuple-element.26), channel_id=1, source_target_pairs={{8,0},{16,8},{24,16},{32,24},{40,32},{48,40},{56,48},{64,56},{72,6... | collective-permute-start | bytes 1544 | tf_op jit(solution)/shard_map/ppermute | solution.py:23
  237.5 7.3 %collective-permute-start.30 = (f32[66,1]{1,0:T(8,128)S(1)}, f32[66,1]{1,0:T(8,128)S(1)}, u32[]{:S(2)}, u32[]{:S(2)}) collective-permute-start(f32[66,1]{1,0:T(8,128)S(1)} %get-tuple-element.9), channel_id=1, source_target_pairs={{1,0},{2,1},{3,2},{4,3},{5,4},{6,5},{7,6},{9,8},{10,9},{11,10},{12... | collective-permute-start | bytes 800 | tf_op jit(solution)/shard_map/ppermute | solution.py:23
  239.4 6.4 %collective-permute-start.31 = (f32[66,1]{1,0:T(8,128)S(1)}, f32[66,1]{1,0:T(8,128)S(1)}, u32[]{:S(2)}, u32[]{:S(2)}) collective-permute-start(f32[66,1]{1,0:T(8,128)S(1)} %get-tuple-element.10), channel_id=1, source_target_pairs={{0,1},{1,2},{2,3},{3,4},{4,5},{5,6},{6,7},{8,9},{9,10},{10,11},{11... | collective-permute-start | bytes 800 | tf_op jit(solution)/shard_map/ppermute | solution.py:20
  246.0 5.1 %collective-permute-start.33 = (f32[1,128]{1,0:T(1,128)S(1)}, f32[1,128]{1,0:T(1,128)S(1)}, u32[]{:S(2)}, u32[]{:S(2)}) collective-permute-start(f32[1,128]{1,0:T(1,128)S(1)} %get-tuple-element.23), channel_id=1, source_target_pairs={{0,8},{8,16},{16,24},{24,32},{32,40},{40,48},{48,56},{56,64},{64,7... | collective-permute-start | bytes 1544 | tf_op jit(solution)/shard_map/ppermute | solution.py:20
  249.7 4.6 %collective-permute-start.32 = (f32[1,128]{1,0:T(1,128)S(1)}, f32[1,128]{1,0:T(1,128)S(1)}, u32[]{:S(2)}, u32[]{:S(2)}) collective-permute-start(f32[1,128]{1,0:T(1,128)S(1)} %get-tuple-element.24), channel_id=1, source_target_pairs={{8,0},{16,8},{24,16},{32,24},{40,32},{48,40},{56,48},{64,56},{72,6... | collective-permute-start | bytes 1544 | tf_op jit(solution)/shard_map/ppermute | solution.py:23
  254.4 7.3 %collective-permute-start.34 = (f32[66,1]{1,0:T(8,128)S(1)}, f32[66,1]{1,0:T(8,128)S(1)}, u32[]{:S(2)}, u32[]{:S(2)}) collective-permute-start(f32[66,1]{1,0:T(8,128)S(1)} %get-tuple-element.7), channel_id=1, source_target_pairs={{1,0},{2,1},{3,2},{4,3},{5,4},{6,5},{7,6},{9,8},{10,9},{11,10},{12... | collective-permute-start | bytes 800 | tf_op jit(solution)/shard_map/ppermute | solution.py:23
  256.3 6.4 %collective-permute-start.35 = (f32[66,1]{1,0:T(8,128)S(1)}, f32[66,1]{1,0:T(8,128)S(1)}, u32[]{:S(2)}, u32[]{:S(2)}) collective-permute-start(f32[66,1]{1,0:T(8,128)S(1)} %get-tuple-element.8), channel_id=1, source_target_pairs={{0,1},{1,2},{2,3},{3,4},{4,5},{5,6},{6,7},{8,9},{9,10},{10,11},{11... | collective-permute-start | bytes 800 | tf_op jit(solution)/shard_map/ppermute | solution.py:20
where the time goes:
time: 266 us; the launch traced here: 263 us
  starting transfers between devices  137 us (52%)
  waiting for transfers between devices  54.3 us (20%)
  local copies, waits for them, and re-layouts  30.2 us (11%)
  blocking collectives  23.4 us (9%)
  matrix products  12.2 us (5%)
  other arithmetic  5.35 us (2%)
    ppermute x18, starting transfers between devices, with_halo(): lax.ppermute(lax.slice_in_dim(block, block.shape[dim] - width, None, axis...  71.1 us
    ppermute x18, starting transfers between devices, with_halo(): lax.ppermute(lax.slice_in_dim(block, 0, width, axis=dim), axis, backward)  33.5 us
    all_to_all x1, blocking collectives, on_device(): lax.all_to_all(fields, 'px', split_axis=1, concat_axis=2, tiled=True)  23.4 us
    ppermute x18, waiting for transfers between devices, with_halo(): lax.ppermute(lax.slice_in_dim(block, 0, width, axis=dim), axis, backward)  22.5 us
    all_to_all x1, waiting for transfers between devices, on_device(): lax.all_to_all(half_step, 'py', split_axis=1, concat_axis=3, tiled=True)  14.5 us
    all_to_all x1, starting transfers between devices, on_device(): lax.all_to_all(sending.astype(jnp.bfloat16), ('px', 'py'), split_axis=0,...  9.76 us
    all_to_all x1, starting transfers between devices, on_device(): lax.all_to_all(half_step, 'py', split_axis=1, concat_axis=3, tiled=True)  8.7 us
    all_to_all x2, starting transfers between devices, on_device(): lax.all_to_all((result[2] + time_step * (-speed * result[0] + rates * res...  8.09 us
  transfers between devices with their start and end apart: 41, of which 18 were waited for; matrix products, arithmetic and copies ran while one was open for 13% of the time, Pallas kernels for 0%

commit v1 on v0

v1 whole, which is shorter than its diff:
```python
import jax
import jax.numpy as jnp
from jax import lax
from jax.experimental import pallas as pl
from jax.experimental.pallas import tpu as pltpu
from jax.sharding import PartitionSpec as P

COND_STEPS = 8
time_step = 0.25
wall_gain = 0.5
diffusion_rate = 0.24
source_gain = 0.1

NPX = 16
NPY = 8
DEV = NPX * NPY
F = 4
NZ = 16
XB = 64
YB = 128
SLOT = 8
HALO = 8
ROWS = XB + 2 * HALO
COLS = 3 * YB
TILE = 256
MESH = pl.DeviceIdType.MESH
BF = jnp.bfloat16
F32 = jnp.float32


def iota(shape, axis):
    return lax.broadcasted_iota(jnp.int32, shape, axis)


def kernel(
    fields,
    xop_hbm,
    yop_hbm,
    visc,
    tile_ref,
    owner_ref,
    row_ref,
    temp_hbm,
    cond_hbm,
    out,
    solid_out,
    xop,
    yop,
    xrows,
    half,
    yrows,
    ysend,
    theta,
    gather,
    place,
    tags,
    wsend,
    wrecv,
    t_ext,
    k_ext,
    s_ext,
    load_sem,
    s1,
    r1,
    s2,
    r2,
    s4,
    r4,
    sw,
    rw,
    sh,
    rh,
    copy_sem,
    all_in,
):
    a = lax.axis_index("px")
    b = lax.axis_index("py")
    me = a * NPY + b
    held = a // 2
    par = a % 2
    is_self = held == b

    bar = pltpu.get_barrier_semaphore()

    @pl.loop(1, NPX)
    def _(d):
        pl.semaphore_signal(
            bar, inc=1, device_id=((a + d) % NPX, b), device_id_type=MESH
        )

    @pl.loop(1, NPY)
    def _(d):
        pl.semaphore_signal(
            bar, inc=1, device_id=(a, (b + d) % NPY), device_id_type=MESH
        )

    xload = pltpu.make_async_copy(xop_hbm, xop, load_sem.at[0])
    yload = pltpu.make_async_copy(yop_hbm, yop, load_sem.at[1])
    xload.start()
    yload.start()

    pl.semaphore_wait(bar, NPX + NPY - 2)

    def send_x(f):
        @pl.loop(1, NPX)
        def _(d):
            t = (a + d) % NPX
            pltpu.make_async_remote_copy(
                src_ref=fields.at[f, t],
                dst_ref=xrows.at[f, pl.ds(a * XB, XB)],
                send_sem=s1.at[f],
                recv_sem=r1.at[f],
                device_id=(t, b),
                device_id_type=MESH,
            ).start()

        pltpu.make_async_copy(
            fields.at[f, a], xrows.at[f, pl.ds(a * XB, XB)], r1.at[f]
        ).start()

    def wait_bytes(ref, sem):
        pltpu.make_async_copy(ref, ref, sem).wait()

    send_x(0)

    @pl.loop(1, NPX)
    def _(d):
        pl.semaphore_signal(
            all_in, inc=1, device_id=((a + d) % NPX, b), device_id_type=MESH
        )

    send_x(1)
    send_x(3)

    own = jnp.broadcast_to(owner_ref[...], (YB, YB))
    match = own == iota((YB, YB), 0)
    upper = (iota((YB, YB), 0) < iota((YB, YB), 1)).astype(F32).astype(BF)
    onehot = match.astype(F32)
    earlier = jnp.dot(onehot.astype(BF), upper, preferred_element_type=F32)
    pos = jnp.sum(earlier * onehot, axis=0, keepdims=True)
    dest = owner_ref[...].astype(F32) * SLOT + pos
    line = iota((DEV * SLOT, YB), 0).astype(F32)
    place[...] = (line == dest).astype(F32).astype(BF)
    tagged = jnp.where(line == dest + 4.0, row_ref[...].astype(F32) + 1.0, 0.0)
    tags[...] = jnp.dot(
        tagged.astype(BF), jnp.ones((YB, YB), BF), preferred_element_type=F32
    )
    tcol = jnp.broadcast_to(tile_ref[...].astype(F32), (YB, YB)).T
    for n in range(NZ * XB // YB):
        gather[:, n * YB : (n + 1) * YB] = (
            (tcol == (iota((YB, YB), 1) + n * YB).astype(F32)).astype(F32).astype(BF)
        )

    pl.semaphore_wait(all_in, NPX - 1)

    def around():
        for dr in (-1, 0, 1):
            for dc in (-1, 0, 1):
                if dr or dc:
                    yield dr, dc

    def halo(src, r0, dst, ssem, rsem):
        for dr, dc in around():
            if dr == 0:
                rows, to = pl.ds(r0, XB), pl.ds(HALO, XB)
            elif dr == 1:
                rows, to = pl.ds(r0 + XB - HALO, HALO), pl.ds(0, HALO)
            else:
                rows, to = pl.ds(r0, HALO), pl.ds(HALO + XB, HALO)
            cols = pl.ds((1 - dc) * YB, YB)
            view = src.at[rows] if r0 == 0 else src.at[rows, pl.ds(YB, YB)]
            pltpu.make_async_remote_copy(
                src_ref=view,
                dst_ref=dst.at[to, cols],
                send_sem=ssem,
                recv_sem=rsem,
                device_id=((a + dr + NPX) % NPX, (b + dc + NPY) % NPY),
                device_id_type=MESH,
            ).start()

    def halo_wait(dst, ssem, rsem, own_block):
        amount = 6 * HALO + 2 * XB
        flat = xrows.at[0, pl.ds(0, 2 * amount)]
        wait_bytes(flat, ssem)
        if own_block:
            amount += XB
        wait_bytes(xrows.at[0, pl.ds(0, 2 * amount)], rsem)

    centre = (pl.ds(HALO, XB), pl.ds(YB, YB))
    halo(temp_hbm, 0, t_ext, sh.at[0], rh.at[0])
    halo(cond_hbm, 0, k_ext, sh.at[1], rh.at[1])
    pltpu.make_async_copy(temp_hbm, t_ext.at[centre], rh.at[0]).start()
    pltpu.make_async_copy(cond_hbm, k_ext.at[centre], rh.at[1]).start()

    def send_half(f, tile):
        @pl.loop(0, TILE // XB)
        def _(j):
            t = tile * (TILE // XB) + j
            src = half.at[f, pl.ds(t * XB, XB)]
            dst = yrows.at[f, b, pl.ds(par * XB, XB)]
            local = jnp.logical_and(is_self, t == a)

            @pl.when(local)
            def _():
                pltpu.make_async_copy(src, dst, r2.at[f]).start()

            @pl.when(jnp.logical_not(local))
            def _():
                pltpu.make_async_remote_copy(
                    src_ref=src,
                    dst_ref=dst,
                    send_sem=s2.at[f],
                    recv_sem=r2.at[f],
                    device_id=(t, held),
                    device_id_type=MESH,
                ).start()

    def tile_x(f, tile):
        rr = pl.ds(pl.multiple_of(tile * TILE, TILE), TILE)
        q = xrows[f]
        r0 = jnp.dot(xop[0, rr, :], q, preferred_element_type=F32)
        r1_ = jnp.dot(xop[1, rr, :], q, preferred_element_type=F32)
        r2_ = jnp.dot(xop[2, rr, :], q, preferred_element_type=F32)
        speed = xrows[0, rr, :].astype(F32)
        half[f, rr, :] = (
            r2_ + time_step * (-speed * r0 + visc[f] * r1_)
        ).astype(BF)

    tiles = NPX * XB // TILE

    def pass_x(f):
        first = a // 4
        tile_x(f, first)

        @pl.loop(1, tiles)
        def _(i):
            tile_x(f, (first + i) % tiles)
            send_half(f, (first + i - 1) % tiles)

        send_half(f, (first + tiles - 1) % tiles)

    def send_y(f, tile):
        for j in range(TILE // YB):
            t = tile * (TILE // YB) + j
            src = ysend.at[f, t]
            if f == 3:
                dst = theta.at[pl.ds(2 * b, 2)]
            else:
                dst = out.at[f, pl.ds(2 * b, 2)]

            @pl.when(t == b)
            def _():
                pltpu.make_async_copy(src, dst, r4.at[f]).start()

            @pl.when(t != b)
            def _():
                pltpu.make_async_remote_copy(
                    src_ref=src,
                    dst_ref=dst,
                    send_sem=s4.at[f],
                    recv_sem=r4.at[f],
                    device_id=(a, t),
                    device_id_type=MESH,
                ).start()

    nt = (((1,), (1,)), ((), ()))

    def tile_y(f, tile):
        rr = pl.ds(pl.multiple_of(tile * TILE, TILE), TILE)
        q = jnp.concatenate([yrows[f, n] for n in range(NPY)], axis=1)
        r0 = lax.dot_general(q, yop[0, rr, :], nt, preferred_element_type=F32)
        r1_ = lax.dot_general(q, yop[1, rr, :], nt, preferred_element_type=F32)
        r2_ = lax.dot_general(q, yop[2, rr, :], nt, preferred_element_type=F32)
        for j in range(TILE // YB):
            t = tile * (TILE // YB) + j
            cc = slice(j * YB, (j + 1) * YB)
            speed = yrows[1, t].astype(F32)
            new = r2_[:, cc] + time_step * (
                -speed * r0[:, cc] + visc[f] * r1_[:, cc]
            )
            ysend[f, t] = new.astype(BF).reshape(2, XB, YB)

    ytiles = NPY * YB // TILE

    def pass_y(f):
        first = b // 2
        tile_y(f, first)

        @pl.loop(1, ytiles)
        def _(i):
            tile_y(f, (first + i) % ytiles)
            send_y(f, (first + i - 1) % ytiles)

        send_y(f, (first + ytiles - 1) % ytiles)

    def got_x(f):
        wait_bytes(xrows.at[f], r1.at[f])

    def got_half(f):
        wait_bytes(yrows.at[f], r2.at[f])

    xload.wait()
    got_x(0)
    got_x(1)
    pass_x(1)
    got_x(3)
    pass_x(3)
    send_x(2)
    pass_x(0)

    halo_wait(t_ext, sh.at[0], rh.at[0], True)
    halo_wait(k_ext, sh.at[1], rh.at[1], True)
    grow = iota((ROWS, COLS), 0) + (a * XB - HALO)
    gcol = iota((ROWS, COLS), 1) + (b * YB - YB)
    inside = (
        (grow >= 0) & (grow < NPX * XB) & (gcol >= 0) & (gcol < NPY * YB)
    )
    k_ext[...] = jnp.where(inside, k_ext[...], 0.0)
    t_ext[...] = jnp.where(inside, t_ext[...], 0.0)

    yload.wait()
    got_half(1)
    got_half(3)
    pass_y(3)
    pass_y(1)
    got_x(2)
    pass_x(2)
    got_half(0)
    pass_y(0)

    wait_bytes(theta, r4.at[3])
    keep_theta = pltpu.make_async_copy(theta, out.at[3], copy_sem)
    keep_theta.start()
    lines = theta[...].reshape(NZ * XB, YB)
    flux = jnp.dot(gather[...], lines, preferred_element_type=F32).astype(BF)
    wsend[...] = (
        jnp.dot(place[...], flux, preferred_element_type=F32) + tags[...]
    ).astype(BF)

    @pl.loop(1, DEV)
    def _(d):
        t = (me + d) % DEV
        pltpu.make_async_remote_copy(
            src_ref=wsend.at[pl.ds(t * SLOT, SLOT)],
            dst_ref=wrecv.at[pl.ds(me * SLOT, SLOT)],
            send_sem=sw,
            recv_sem=rw,
            device_id=(t // NPY, t % NPY),
            device_id_type=MESH,
        ).start()

    pltpu.make_async_copy(
        wsend.at[pl.ds(me * SLOT, SLOT)], wrecv.at[pl.ds(me * SLOT, SLOT)], rw
    ).start()

    got_half(2)
    pass_y(2)

    wait_bytes(wrecv, rw)
    arrived = wrecv[...]
    named = pltpu.roll(arrived.astype(F32), DEV * SLOT - 4, 0)
    mine = iota((DEV * SLOT, YB), 0) % SLOT < 4
    select = jnp.where(
        mine & (named == (iota((DEV * SLOT, YB), 1) + 1).astype(F32)), 1.0, 0.0
    ).astype(BF)
    source = lax.dot_general(
        select, arrived, (((0,), (0,)), ((), ())), preferred_element_type=F32
    )[:XB]
    s_ext[HALO : HALO + XB, YB : 2 * YB] = source * (source_gain * wall_gain)

    kappa = k_ext[...]

    def north(v):
        return pltpu.roll(v, 1, 0)

    def south(v):
        return pltpu.roll(v, ROWS - 1, 0)

    def west(v):
        return pltpu.roll(v, 1, 1)

    def east(v):
        return pltpu.roll(v, COLS - 1, 1)

    rate = 0.5 * diffusion_rate
    sides = (north, south, west, east)
    coef = [
        jnp.where(inside, rate * (kappa + side(kappa)), 0.0) for side in sides
    ]
    stay = 1.0 - (coef[0] + coef[1] + coef[2] + coef[3])

    halo(s_ext, HALO, s_ext, sh.at[2], rh.at[2])
    halo_wait(s_ext, sh.at[2], rh.at[2], False)

    heat = jnp.where(inside, s_ext[...], 0.0)
    temp = t_ext[...]
    for _ in range(COND_STEPS):
        new = stay * temp + heat
        for c, side in zip(coef, sides):
            new = new + c * side(temp)
        temp = new
    solid_out[...] = temp[HALO : HALO + XB, YB : 2 * YB]

    for f in range(3):
        wait_bytes(out.at[f], r4.at[f])
    keep_theta.wait()
    for f in range(F):
        wait_bytes(xrows.at[f, pl.ds(0, XB * (NPX - 1))], s1.at[f])

        @pl.when(is_self)
        def _():
            wait_bytes(half.at[f, pl.ds(0, XB * (NPX - 1))], s2.at[f])

        @pl.when(jnp.logical_not(is_self))
        def _():
            wait_bytes(half.at[f], s2.at[f])

        wait_bytes(ysend.at[f, pl.ds(0, NPY - 1)], s4.at[f])
    wait_bytes(wsend.at[pl.ds(0, (DEV - 1) * SLOT)], sw)


def on_device(
    fields,
    x_operators,
    y_operators,
    viscosity,
    wall_tile,
    wall_owner,
    wall_row,
    solid_temp,
    conductivity,
):
    any_ = pl.BlockSpec(memory_space=pl.ANY)
    vmem = pl.BlockSpec(memory_space=pltpu.VMEM)
    smem = pl.BlockSpec(memory_space=pltpu.SMEM)
    dma = pltpu.SemaphoreType.DMA
    new_fields, new_solid = pl.pallas_call(
        kernel,
        out_shape=(
            jax.ShapeDtypeStruct(fields.shape, BF),
            jax.ShapeDtypeStruct(solid_temp.shape, F32),
        ),
        in_specs=[any_, any_, any_, smem, vmem, vmem, vmem, any_, any_],
        out_specs=(any_, vmem),
        scratch_shapes=[
            pltpu.VMEM((3, NPX * XB, NPX * XB), BF),
            pltpu.VMEM((3, NPY * YB, NPY * YB), BF),
            pltpu.VMEM((F, NPX * XB, YB), BF),
            pltpu.VMEM((F, NPX * XB, YB), BF),
            pltpu.VMEM((F, NPY, 2 * XB, YB), BF),
            pltpu.VMEM((F, NPY, 2, XB, YB), BF),
            pltpu.VMEM((NZ, XB, YB), BF),
            pltpu.VMEM((YB, NZ * XB), BF),
            pltpu.VMEM((DEV * SLOT, YB), BF),
            pltpu.VMEM((DEV * SLOT, YB), F32),
            pltpu.VMEM((DEV * SLOT, YB), BF),
            pltpu.VMEM((DEV * SLOT, YB), BF),
            pltpu.VMEM((ROWS, COLS), F32),
            pltpu.VMEM((ROWS, COLS), F32),
            pltpu.VMEM((ROWS, COLS), F32),
            dma((2,)),
            dma((F,)),
            dma((F,)),
            dma((F,)),
            dma((F,)),
            dma((F,)),
            dma((F,)),
            dma,
            dma,
            dma((3,)),
            dma((3,)),
            dma,
            pltpu.SemaphoreType.REGULAR,
        ],
        compiler_params=pltpu.CompilerParams(
            collective_id=0, has_side_effects=True, vmem_limit_bytes=48 << 20
        ),
        name="substep",
    )(
        fields,
        x_operators,
        y_operators,
        viscosity,
        wall_tile.reshape(1, -1),
        wall_owner.reshape(1, -1),
        wall_row.reshape(1, -1),
        solid_temp,
        conductivity,
    )
    return new_fields, new_solid


def solution(mesh):
    return jax.shard_map(
        on_device,
        mesh=mesh,
        in_specs=(
            P(None, None, "px", "py"),
            P(),
            P(),
            P(),
            P(("px", "py")),
            P(("px", "py"), None),
            P(("px", "py")),
            P("px", "py"),
            P("px", "py"),
        ),
        out_specs=(P(None, None, "px", "py"), P("px", "py")),
        check_vma=False,
    )
```

time: 266 us -> 66.4 us (0.25)
  starting transfers between devices: 137 us -> 0 us
  Pallas kernels: 0 us -> 58.5 us
  waiting for transfers between devices: 54.3 us -> 0 us
  blocking collectives: 23.4 us -> 0 us
  local copies, waits for them, and re-layouts: 30.2 us -> 6.94 us
  matrix products: 12.2 us -> 0 us
  other arithmetic: 5.35 us -> 0 us
    ppermute x36 -> x0, starting transfers between devices: 105 us -> none  [the longest x18 71.1 us: with_halo(): lax.ppermute(lax.slice_in_dim(block, block.shape[dim] - width, None, axis...]
    pallas_call x0 -> x1, Pallas kernels: none -> 58.5 us  [on_device(): pl.pallas_call(kernel, out_shape=(jax.ShapeDtypeStruct(fields.shape, BF),...]
    all_to_all x5 -> x0, starting transfers between devices: 32 us -> none  [the longest x1 9.76 us: on_device(): lax.all_to_all(sending.astype(jnp.bfloat16), ('px', 'py'), split_axis=0,...]
    ppermute x36 -> x0, waiting for transfers between devices: 29.8 us -> none  [the longest x18 22.5 us: with_halo(): lax.ppermute(lax.slice_in_dim(block, 0, width, axis=dim), axis, backward)]
    all_to_all x5 -> x0, waiting for transfers between devices: 24.4 us -> none  [the longest x1 14.5 us: on_device(): lax.all_to_all(half_step, 'py', split_axis=1, concat_axis=3, tiled=True)]
    all_to_all x1 -> x0, blocking collectives: 23.4 us -> none  [on_device(): lax.all_to_all(fields, 'px', split_axis=1, concat_axis=2, tiled=True)]
    scatter x2 -> x0, local copies, waits for them, and re-layouts: 12.9 us -> none  [the longest x1 6.55 us: on_device(): jnp.zeros((devices, capacity, width), jnp.float32).at[owner, position]]
    dot_general x3 -> x0, matrix products: 12.2 us -> none  [the longest x1 5.67 us: on_device(): jnp.einsum('oij,fzjy->ofziy', x_operators, x_rows, preferred_element_type...]
  transfers between devices with their start and end apart: 41 -> 0, of which waited for: 18 -> 0; matrix products, arithmetic and copies ran while one was open for 13% -> 0% of each run, Pallas kernels for 0% -> 0%
where the time goes in v1:
time: 66.4 us; the launch traced here: 66.1 us
  Pallas kernels  58.5 us (88%)
  local copies, waits for them, and re-layouts  6.94 us (10%)
    pallas_call x1, Pallas kernels, on_device(): pl.pallas_call(kernel, out_shape=(jax.ShapeDtypeStruct(fields.shape, BF),...  58.5 us
    unnamed x16, local copies, waits for them, and re-layouts  6.94 us

profile of v1, /device:TPU:1, one launch (start us, length us, event | category | flops | bytes accessed | tf_op | source)
XLA Modules:
  0.0 66.1 jit_solution(4438463521020647692)
XLA Ops:
  0.6 0.0 copy-start
  0.6 1.2 %copy-done = bf16[4,16,64,128]{3,2,1,0:T(8,128)(2,1)S(1)} copy-done((bf16[4,16,64,128]{3,2,1,0:T(8,128)(2,1)S(1)}, bf16[4,16,64,128]{3,2,1,0:T(8,128)(2,1)}, u32[]{:S(2)}) %copy-start) | copy-done | bytes 1048600
  1.9 0.0 copy-start.1
  1.9 0.8 %copy-done.1 = f32[64,128]{1,0:T(8,128)S(1)} copy-done((f32[64,128]{1,0:T(8,128)S(1)}, f32[64,128]{1,0:T(8,128)}, u32[]{:S(2)}) %copy-start.1) | copy-done | bytes 32792
  2.6 0.0 copy-start.2
  2.6 0.8 %copy-done.2 = f32[64,128]{1,0:T(8,128)S(1)} copy-done((f32[64,128]{1,0:T(8,128)S(1)}, f32[64,128]{1,0:T(8,128)}, u32[]{:S(2)}) %copy-start.2) | copy-done | bytes 32792
  3.4 0.0 copy-start.3
  3.4 0.7 copy-done.3
  4.0 0.0 copy-start.4
  4.0 0.7 copy-done.4
  4.7 0.0 copy-start.5
  4.7 0.7 copy-done.5
  5.3 0.0 copy-start.6
  5.3 0.7 copy-done.6
  6.0 58.5 %substep.1 = (bf16[4,16,64,128]{3,2,1,0:T(8,128)(2,1)S(1)}, f32[64,128]{1,0:T(8,128)S(1)}) custom-call(bf16[4,16,64,128]{3,2,1,0:T(8,128)(2,1)S(1)} %copy-done, bf16[3,1024,1024]{2,1,0:T(8,128)(2,1)} %xop_hbm.1, bf16[3,1024,1024]{2,1,0:T(8,128)(2,1)} %yop_hbm.1, f32[4]{0:T(128)S(1)} %copy-done.3, s32[1,128]{1,0:T(1,128)S(1)} %bitcast.3, ...), custom_call_target="tpu_custom_call" | custom-call | tf_op jit(solution)/shard_map/substep/pallas_call | solution.py:437
  64.5 1.0 %copy.13 = bf16[4,16,64,128]{3,2,1,0:T(8,128)(2,1)} copy(bf16[4,16,64,128]{3,2,1,0:T(8,128)(2,1)S(1)} %get-tuple-element.4) | data formatting | bytes 2097152
  65.5 0.6 copy.14
Async XLA Ops:
  0.6 1.2 %copy-start = (bf16[4,16,64,128]{3,2,1,0:T(8,128)(2,1)S(1)}, bf16[4,16,64,128]{3,2,1,0:T(8,128)(2,1)}, u32[]{:S(2)}) copy-start(bf16[4,16,64,128]{3,2,1,0:T(8,128)(2,1)} %fields.1) | copy-start | bytes 3145732
  1.9 0.8 %copy-start.1 = (f32[64,128]{1,0:T(8,128)S(1)}, f32[64,128]{1,0:T(8,128)}, u32[]{:S(2)}) copy-start(f32[64,128]{1,0:T(8,128)} %temp_hbm.1) | copy-start | bytes 98308
  2.6 0.8 %copy-start.2 = (f32[64,128]{1,0:T(8,128)S(1)}, f32[64,128]{1,0:T(8,128)}, u32[]{:S(2)}) copy-start(f32[64,128]{1,0:T(8,128)} %cond_hbm.1) | copy-start | bytes 98308
  3.4 0.7 copy-start.3
  4.0 0.7 copy-start.4
  4.7 0.7 copy-start.5
  5.3 0.7 copy-start.6

commit v2 on v1

--- a/solution.py
+++ b/solution.py
@@ -18,7 +18,9 @@
 NZ = 16
 XB = 64
 YB = 128
-SLOT = 8
+CAP = 4
+LINES = NPX * CAP
+SLOTS = DEV * CAP
 HALO = 8
 ROWS = XB + 2 * HALO
 COLS = 3 * YB
@@ -36,16 +38,22 @@
     fields,
     xop_hbm,
     yop_hbm,
+    visc_hbm,
+    tile_hbm,
+    owner_hbm,
+    row_hbm,
+    temp_hbm,
+    cond_hbm,
+    out,
+    solid_out,
     visc,
     tile_ref,
     owner_ref,
     row_ref,
-    temp_hbm,
-    cond_hbm,
-    out,
-    solid_out,
+    solid,
     xop,
     yop,
+    yopt,
     xrows,
     half,
     yrows,
@@ -53,12 +61,20 @@
     theta,
     gather,
     place,
-    tags,
+    perm,
+    select,
+    tsend,
+    tmid,
+    tturn,
+    ttag,
     wsend,
+    wmid,
+    wturn,
     wrecv,
     t_ext,
     k_ext,
     s_ext,
+    coef,
     load_sem,
     s1,
     r1,
@@ -96,6 +112,19 @@
 
     xload = pltpu.make_async_copy(xop_hbm, xop, load_sem.at[0])
     yload = pltpu.make_async_copy(yop_hbm, yop, load_sem.at[1])
+    small = [
+        pltpu.make_async_copy(src, dst, load_sem.at[2 + n])
+        for n, (src, dst) in enumerate(
+            (
+                (visc_hbm, visc),
+                (tile_hbm, tile_ref),
+                (owner_hbm, owner_ref),
+                (row_hbm, row_ref),
+            )
+        )
+    ]
+    for load in small:
+        load.start()
     xload.start()
     yload.start()
 
@@ -132,18 +161,73 @@
     send_x(1)
     send_x(3)
 
+    for load in small:
+        load.wait()
     own = jnp.broadcast_to(owner_ref[...], (YB, YB))
     match = own == iota((YB, YB), 0)
     upper = (iota((YB, YB), 0) < iota((YB, YB), 1)).astype(F32).astype(BF)
     onehot = match.astype(F32)
     earlier = jnp.dot(onehot.astype(BF), upper, preferred_element_type=F32)
     pos = jnp.sum(earlier * onehot, axis=0, keepdims=True)
-    dest = owner_ref[...].astype(F32) * SLOT + pos
-    line = iota((DEV * SLOT, YB), 0).astype(F32)
-    place[...] = (line == dest).astype(F32).astype(BF)
-    tagged = jnp.where(line == dest + 4.0, row_ref[...].astype(F32) + 1.0, 0.0)
-    tags[...] = jnp.dot(
-        tagged.astype(BF), jnp.ones((YB, YB), BF), preferred_element_type=F32
+    owner = owner_ref[...]
+    to_a = (owner // NPY).astype(F32) * CAP + pos
+    to_b = (owner % NPY).astype(F32)
+    dest = to_b * LINES + to_a
+    place[...] = (iota((SLOTS, YB), 0).astype(F32) == dest).astype(F32).astype(BF)
+    name = row_ref[...].astype(F32) + 1.0
+    named = jnp.where(
+        (iota((NPY * 8, YB), 0) // 8).astype(F32) == to_b, name, 0.0
+    ).astype(BF)
+    spot = (iota((YB, YB), 0).astype(F32) == to_a).astype(F32).astype(BF)
+    tsend[...] = lax.dot_general(
+        named, spot, (((1,), (1,)), ((), ())), preferred_element_type=F32
+    ).astype(BF)
+
+    def along_y(src, dst, size, n):
+        @pl.loop(1, NPY)
+        def _(d):
+            t = (b + d) % NPY
+            pltpu.make_async_remote_copy(
+                src_ref=src.at[pl.ds(t * size, size)],
+                dst_ref=dst.at[pl.ds(b * size, size)],
+                send_sem=sw.at[n],
+                recv_sem=rw.at[n],
+                device_id=(a, t),
+                device_id_type=MESH,
+            ).start()
+
+        pltpu.make_async_copy(
+            src.at[pl.ds(b * size, size)], dst.at[pl.ds(b * size, size)], rw.at[n]
+        ).start()
+
+    def along_x(src, dst, size, n):
+        @pl.loop(1, NPX)
+        def _(d):
+            t = (a + d) % NPX
+            pltpu.make_async_remote_copy(
+                src_ref=src.at[pl.ds(t * size, size)],
+                dst_ref=dst.at[pl.ds(a * size, size)],
+                send_sem=sw.at[n],
+                recv_sem=rw.at[n],
+                device_id=(t, b),
+                device_id_type=MESH,
+            ).start()
+
+        pltpu.make_async_copy(
+            src.at[pl.ds(a * size, size)], dst.at[pl.ds(a * size, size)], rw.at[n]
+        ).start()
+
+    along_y(tsend, tmid, 8, 2)
+    r_to = iota((SLOTS, SLOTS), 0)
+    perm[...] = (
+        (
+            iota((SLOTS, SLOTS), 1)
+            == ((r_to % (NPY * CAP)) // CAP) * LINES
+            + (r_to // (NPY * CAP)) * CAP
+            + r_to % CAP
+        )
+        .astype(F32)
+        .astype(BF)
     )
     tcol = jnp.broadcast_to(tile_ref[...].astype(F32), (YB, YB)).T
     for n in range(NZ * XB // YB):
@@ -228,16 +312,22 @@
 
     tiles = NPX * XB // TILE
 
+    def far_first(i):
+        return (2 - i) * (1 - i // 2) + 3 * (3 - i) * (i // 2)
+
+
     def pass_x(f):
-        first = a // 4
-        tile_x(f, first)
+        def turn(i):
+            return (a // 4 + far_first(i)) % tiles
+
+        tile_x(f, turn(0))
 
         @pl.loop(1, tiles)
         def _(i):
-            tile_x(f, (first + i) % tiles)
-            send_half(f, (first + i - 1) % tiles)
-
-        send_half(f, (first + tiles - 1) % tiles)
+            tile_x(f, turn(i))
+            send_half(f, turn(i - 1))
+
+        send_half(f, turn(tiles - 1))
 
     def send_y(f, tile):
         for j in range(TILE // YB):
@@ -263,14 +353,12 @@
                     device_id_type=MESH,
                 ).start()
 
-    nt = (((1,), (1,)), ((), ()))
-
     def tile_y(f, tile):
         rr = pl.ds(pl.multiple_of(tile * TILE, TILE), TILE)
         q = jnp.concatenate([yrows[f, n] for n in range(NPY)], axis=1)
-        r0 = lax.dot_general(q, yop[0, rr, :], nt, preferred_element_type=F32)
-        r1_ = lax.dot_general(q, yop[1, rr, :], nt, preferred_element_type=F32)
-        r2_ = lax.dot_general(q, yop[2, rr, :], nt, preferred_element_type=F32)
+        r0 = jnp.dot(q, yopt[0, :, rr], preferred_element_type=F32)
+        r1_ = jnp.dot(q, yopt[1, :, rr], preferred_element_type=F32)
+        r2_ = jnp.dot(q, yopt[2, :, rr], preferred_element_type=F32)
         for j in range(TILE // YB):
             t = tile * (TILE // YB) + j
             cc = slice(j * YB, (j + 1) * YB)
@@ -283,21 +371,52 @@
     ytiles = NPY * YB // TILE
 
     def pass_y(f):
-        first = b // 2
-        tile_y(f, first)
+        def turn(i):
+            return (b // 2 + far_first(i)) % ytiles
+
+        tile_y(f, turn(0))
 
         @pl.loop(1, ytiles)
         def _(i):
-            tile_y(f, (first + i) % ytiles)
-            send_y(f, (first + i - 1) % ytiles)
-
-        send_y(f, (first + ytiles - 1) % ytiles)
+            tile_y(f, turn(i))
+            send_y(f, turn(i - 1))
+
+        send_y(f, turn(ytiles - 1))
 
     def got_x(f):
         wait_bytes(xrows.at[f], r1.at[f])
 
     def got_half(f):
         wait_bytes(yrows.at[f], r2.at[f])
+
+    yload.wait()
+
+    @pl.loop(0, NPY * YB // TILE)
+    def _(n):
+        rr = pl.ds(pl.multiple_of(n * TILE, TILE), TILE)
+        for k in range(3):
+            for j in range(NPY * YB // TILE):
+                cc = slice(j * TILE, (j + 1) * TILE)
+                yopt[k, cc, rr] = yop[k, rr, cc].T
+
+    wait_bytes(tmid, rw.at[2])
+    lane = iota((NPY * 8, YB), 1)
+    from_b = iota((NPY * 8, YB), 0)
+    pick = (from_b == ((lane % 32) // CAP) * 8) & (lane // 32 == a % 4)
+    cross = lax.dot_general(
+        tmid[...],
+        pick.astype(F32).astype(BF),
+        (((0,), (0,)), ((), ())),
+        preferred_element_type=F32,
+    )
+    same = iota((YB, YB), 0) % CAP == iota((YB, YB), 1) % CAP
+    group = iota((YB, YB), 0) // 8 == iota((YB, YB), 1) // CAP
+    tturn[...] = jnp.dot(
+        group.astype(F32).astype(BF),
+        jnp.where(same, cross, 0.0).astype(BF),
+        preferred_element_type=F32,
+    ).astype(BF)
+    along_x(tturn, ttag, 8, 3)
 
     xload.wait()
     got_x(0)
@@ -305,8 +424,19 @@
     pass_x(1)
     got_x(3)
     pass_x(3)
+    pass_x(0)
     send_x(2)
-    pass_x(0)
+
+    wait_bytes(ttag, rw.at[3])
+    for n in range(SLOTS // YB):
+        tag = jnp.zeros((8, YB), F32)
+        for k in range(4):
+            tag = tag + ttag[(4 * n + k) * 8 : (4 * n + k + 1) * 8, :].astype(F32)
+        select[:, n * YB : (n + 1) * YB] = (
+            (jnp.broadcast_to(tag[:1], (XB, YB)) == (iota((XB, YB), 0) + 1).astype(F32))
+            .astype(F32)
+            .astype(BF)
+        )
 
     halo_wait(t_ext, sh.at[0], rh.at[0], True)
     halo_wait(k_ext, sh.at[1], rh.at[1], True)
@@ -315,79 +445,58 @@
     inside = (
         (grow >= 0) & (grow < NPX * XB) & (gcol >= 0) & (gcol < NPY * YB)
     )
-    k_ext[...] = jnp.where(inside, k_ext[...], 0.0)
+    kappa = jnp.where(inside, k_ext[...], 0.0)
     t_ext[...] = jnp.where(inside, t_ext[...], 0.0)
 
-    yload.wait()
+    def north(v):
+        return pltpu.roll(v, 1, 0)
+
+    def south(v):
+        return pltpu.roll(v, ROWS - 1, 0)
+
+    def west(v):
+        return pltpu.roll(v, 1, 1)
+
+    def east(v):
+        return pltpu.roll(v, COLS - 1, 1)
+
+    rate = 0.5 * diffusion_rate
+    sides = (north, south, west, east)
+    total = jnp.zeros((ROWS, COLS), F32)
+    for n, side in enumerate(sides):
+        part = jnp.where(inside, rate * (kappa + side(kappa)), 0.0)
+        coef[1 + n] = part
+        total = total + part
+    coef[0] = 1.0 - total
+
+
     got_half(1)
     got_half(3)
     pass_y(3)
     pass_y(1)
-    got_x(2)
-    pass_x(2)
-    got_half(0)
-    pass_y(0)
 
     wait_bytes(theta, r4.at[3])
     keep_theta = pltpu.make_async_copy(theta, out.at[3], copy_sem)
     keep_theta.start()
     lines = theta[...].reshape(NZ * XB, YB)
     flux = jnp.dot(gather[...], lines, preferred_element_type=F32).astype(BF)
-    wsend[...] = (
-        jnp.dot(place[...], flux, preferred_element_type=F32) + tags[...]
-    ).astype(BF)
-
-    @pl.loop(1, DEV)
-    def _(d):
-        t = (me + d) % DEV
-        pltpu.make_async_remote_copy(
-            src_ref=wsend.at[pl.ds(t * SLOT, SLOT)],
-            dst_ref=wrecv.at[pl.ds(me * SLOT, SLOT)],
-            send_sem=sw,
-            recv_sem=rw,
-            device_id=(t // NPY, t % NPY),
-            device_id_type=MESH,
-        ).start()
-
-    pltpu.make_async_copy(
-        wsend.at[pl.ds(me * SLOT, SLOT)], wrecv.at[pl.ds(me * SLOT, SLOT)], rw
-    ).start()
-
+    wsend[...] = jnp.dot(place[...], flux, preferred_element_type=F32).astype(BF)
+    along_y(wsend, wmid, LINES, 0)
+
+    got_x(2)
+    pass_x(2)
+    wait_bytes(wmid, rw.at[0])
+    wturn[...] = jnp.dot(perm[...], wmid[...], preferred_element_type=F32).astype(BF)
+    along_x(wturn, wrecv, NPY * CAP, 1)
+
+    got_half(0)
+    pass_y(0)
     got_half(2)
     pass_y(2)
 
-    wait_bytes(wrecv, rw)
-    arrived = wrecv[...]
-    named = pltpu.roll(arrived.astype(F32), DEV * SLOT - 4, 0)
-    mine = iota((DEV * SLOT, YB), 0) % SLOT < 4
-    select = jnp.where(
-        mine & (named == (iota((DEV * SLOT, YB), 1) + 1).astype(F32)), 1.0, 0.0
-    ).astype(BF)
-    source = lax.dot_general(
-        select, arrived, (((0,), (0,)), ((), ())), preferred_element_type=F32
-    )[:XB]
+    wait_bytes(wrecv, rw.at[1])
+    source = jnp.dot(select[...], wrecv[...], preferred_element_type=F32)
     s_ext[HALO : HALO + XB, YB : 2 * YB] = source * (source_gain * wall_gain)
-
-    kappa = k_ext[...]
-
-    def north(v):
-        return pltpu.roll(v, 1, 0)
-
-    def south(v):
-        return pltpu.roll(v, ROWS - 1, 0)
-
-    def west(v):
-        return pltpu.roll(v, 1, 1)
-
-    def east(v):
-        return pltpu.roll(v, COLS - 1, 1)
-
-    rate = 0.5 * diffusion_rate
-    sides = (north, south, west, east)
-    coef = [
-        jnp.where(inside, rate * (kappa + side(kappa)), 0.0) for side in sides
-    ]
-    stay = 1.0 - (coef[0] + coef[1] + coef[2] + coef[3])
 
     halo(s_ext, HALO, s_ext, sh.at[2], rh.at[2])
     halo_wait(s_ext, sh.at[2], rh.at[2], False)
@@ -395,15 +504,18 @@
     heat = jnp.where(inside, s_ext[...], 0.0)
     temp = t_ext[...]
     for _ in range(COND_STEPS):
-        new = stay * temp + heat
-        for c, side in zip(coef, sides):
-            new = new + c * side(temp)
+        new = coef[0] * temp + heat
+        for n, side in enumerate(sides):
+            new = new + coef[1 + n] * side(temp)
         temp = new
-    solid_out[...] = temp[HALO : HALO + XB, YB : 2 * YB]
+    solid[...] = temp[HALO : HALO + XB, YB : 2 * YB]
+    keep_solid = pltpu.make_async_copy(solid, solid_out, load_sem.at[0])
+    keep_solid.start()
 
     for f in range(3):
         wait_bytes(out.at[f], r4.at[f])
     keep_theta.wait()
+    keep_solid.wait()
     for f in range(F):
         wait_bytes(xrows.at[f, pl.ds(0, XB * (NPX - 1))], s1.at[f])
 
@@ -416,7 +528,31 @@
             wait_bytes(half.at[f], s2.at[f])
 
         wait_bytes(ysend.at[f, pl.ds(0, NPY - 1)], s4.at[f])
-    wait_bytes(wsend.at[pl.ds(0, (DEV - 1) * SLOT)], sw)
+    wait_bytes(wsend.at[pl.ds(0, (NPY - 1) * LINES)], sw.at[0])
+    wait_bytes(wturn.at[pl.ds(0, (NPX - 1) * NPY * CAP)], sw.at[1])
+    wait_bytes(tsend.at[pl.ds(0, (NPY - 1) * 8)], sw.at[2])
+    wait_bytes(tturn.at[pl.ds(0, (NPX - 1) * 8)], sw.at[3])
+
+
+def finish(fields_in, solid_in, fields_out, solid_out, held, solid, sem_in, sem_out):
+    pieces = [
+        (fields_in.at[f], held.at[f], fields_out.at[f]) for f in range(F)
+    ] + [(solid_in, solid, solid_out)]
+    loads = [
+        pltpu.make_async_copy(src, mid, sem_in.at[n])
+        for n, (src, mid, _) in enumerate(pieces)
+    ]
+    stores = [
+        pltpu.make_async_copy(mid, dst, sem_out.at[n])
+        for n, (_, mid, dst) in enumerate(pieces)
+    ]
+    for load in loads:
+        load.start()
+    for load, store in zip(loads, stores):
+        load.wait()
+        store.start()
+    for store in stores:
+        store.wait()
 
 
 def on_device(
@@ -430,9 +566,7 @@
     solid_temp,
     conductivity,
 ):
-    any_ = pl.BlockSpec(memory_space=pl.ANY)
-    vmem = pl.BlockSpec(memory_space=pltpu.VMEM)
-    smem = pl.BlockSpec(memory_space=pltpu.SMEM)
+    hbm = pl.BlockSpec(memory_space=pltpu.HBM)
     dma = pltpu.SemaphoreType.DMA
     new_fields, new_solid = pl.pallas_call(
         kernel,
@@ -440,10 +574,16 @@
             jax.ShapeDtypeStruct(fields.shape, BF),
             jax.ShapeDtypeStruct(solid_temp.shape, F32),
         ),
-        in_specs=[any_, any_, any_, smem, vmem, vmem, vmem, any_, any_],
-        out_specs=(any_, vmem),
+        in_specs=[hbm] * 9,
+        out_specs=(hbm, hbm),
         scratch_shapes=[
+            pltpu.SMEM((F,), F32),
+            pltpu.VMEM((1, YB), jnp.int32),
+            pltpu.VMEM((1, YB), jnp.int32),
+            pltpu.VMEM((1, YB), jnp.int32),
+            pltpu.VMEM((XB, YB), F32),
             pltpu.VMEM((3, NPX * XB, NPX * XB), BF),
+            pltpu.VMEM((3, NPY * YB, NPY * YB), BF),
             pltpu.VMEM((3, NPY * YB, NPY * YB), BF),
             pltpu.VMEM((F, NPX * XB, YB), BF),
             pltpu.VMEM((F, NPX * XB, YB), BF),
@@ -451,29 +591,37 @@
             pltpu.VMEM((F, NPY, 2, XB, YB), BF),
             pltpu.VMEM((NZ, XB, YB), BF),
             pltpu.VMEM((YB, NZ * XB), BF),
-            pltpu.VMEM((DEV * SLOT, YB), BF),
-            pltpu.VMEM((DEV * SLOT, YB), F32),
-            pltpu.VMEM((DEV * SLOT, YB), BF),
-            pltpu.VMEM((DEV * SLOT, YB), BF),
+            pltpu.VMEM((SLOTS, YB), BF),
+            pltpu.VMEM((SLOTS, SLOTS), BF),
+            pltpu.VMEM((XB, SLOTS), BF),
+            pltpu.VMEM((NPY * 8, YB), BF),
+            pltpu.VMEM((NPY * 8, YB), BF),
+            pltpu.VMEM((NPX * 8, YB), BF),
+            pltpu.VMEM((NPX * 8, YB), BF),
+            pltpu.VMEM((SLOTS, YB), BF),
+            pltpu.VMEM((SLOTS, YB), BF),
+            pltpu.VMEM((SLOTS, YB), BF),
+            pltpu.VMEM((SLOTS, YB), BF),
             pltpu.VMEM((ROWS, COLS), F32),
             pltpu.VMEM((ROWS, COLS), F32),
             pltpu.VMEM((ROWS, COLS), F32),
-            dma((2,)),
+            pltpu.VMEM((5, ROWS, COLS), F32),
+            dma((6,)),
             dma((F,)),
             dma((F,)),
             dma((F,)),
             dma((F,)),
             dma((F,)),
             dma((F,)),
-            dma,
-            dma,
+            dma((4,)),
+            dma((4,)),
             dma((3,)),
             dma((3,)),
             dma,
             pltpu.SemaphoreType.REGULAR,
         ],
         compiler_params=pltpu.CompilerParams(
-            collective_id=0, has_side_effects=True, vmem_limit_bytes=48 << 20
+            collective_id=0, has_side_effects=True, vmem_limit_bytes=67_043_328
         ),
         name="substep",
     )(
@@ -487,7 +635,23 @@
         solid_temp,
         conductivity,
     )
-    return new_fields, new_solid
+    return pl.pallas_call(
+        finish,
+        out_shape=(
+            jax.ShapeDtypeStruct(fields.shape, BF),
+            jax.ShapeDtypeStruct(solid_temp.shape, F32),
+        ),
+        in_specs=[hbm] * 2,
+        out_specs=(hbm, hbm),
+        scratch_shapes=[
+            pltpu.VMEM((F, NZ, XB, YB), BF),
+            pltpu.VMEM((XB, YB), F32),
+            dma((F + 1,)),
+            dma((F + 1,)),
+        ],
+        compiler_params=pltpu.CompilerParams(vmem_limit_bytes=67_043_328),
+        name="finish",
+    )(new_fields, new_solid)
 
 
 def solution(mesh):

time: 66.4 us -> 57.1 us (0.86)
  local copies, waits for them, and re-layouts: 6.94 us -> 0 us
  Pallas kernels: 58.5 us -> 56.3 us
    unnamed x16 -> x0, local copies, waits for them, and re-layouts: 6.94 us -> none
    pallas_call x1, Pallas kernels: 58.5 us -> 54.3 us  [on_device(): pl.pallas_call(kernel, out_shape=(jax.ShapeDtypeStruct(fields.shape, BF),...]
    pallas_call x0 -> x1, Pallas kernels: none -> 2 us  [on_device(): pl.pallas_call(finish, out_shape=(jax.ShapeDtypeStruct(fields.shape, BF),...]
where the time goes in v2:
time: 57.1 us; the launch traced here: 56.9 us
  Pallas kernels  56.3 us (99%)
  between operations  0.64 us (1%)
    pallas_call x1, Pallas kernels, on_device(): pl.pallas_call(kernel, out_shape=(jax.ShapeDtypeStruct(fields.shape, BF),...  54.3 us
    pallas_call x1, Pallas kernels, on_device(): pl.pallas_call(finish, out_shape=(jax.ShapeDtypeStruct(fields.shape, BF),...  2 us

profile of v2, /device:TPU:1, one launch (start us, length us, event | category | flops | bytes accessed | tf_op | source)
XLA Modules:
  0.0 56.9 jit_solution(3241340888739175580)
XLA Ops:
  0.6 54.3 %substep.1 = (bf16[4,16,64,128]{3,2,1,0:T(8,128)(2,1)}, f32[64,128]{1,0:T(8,128)}) custom-call(bf16[4,16,64,128]{3,2,1,0:T(8,128)(2,1)} %fields.1, bf16[3,1024,1024]{2,1,0:T(8,128)(2,1)} %xop_hbm.1, bf16[3,1024,1024]{2,1,0:T(8,128)(2,1)} %yop_hbm.1, f32[4]{0:T(128)} %visc_hbm.1, s32[1,128]{1,0:T(1,128)} %bitcast.3, s32[1,128]{1,0:T(1,128)} %bitcast.4, ...), custom_call_target="tpu_custom_call" | custom-call | tf_op jit(solution)/shard_map/substep/pallas_call | solution.py:571
  54.9 2.0 %finish.1 = (bf16[4,16,64,128]{3,2,1,0:T(8,128)(2,1)}, f32[64,128]{1,0:T(8,128)}) custom-call(bf16[4,16,64,128]{3,2,1,0:T(8,128)(2,1)} %get-tuple-element.4.fields_in, f32[64,128]{1,0:T(8,128)} %get-tuple-element.5.solid_in), custom_call_target="tpu_custom_call" | custom-call | tf_op jit(solution)/shard_map/finish/pallas_call | solution.py:638

commit v3 on v2

--- a/solution.py
+++ b/solution.py
@@ -61,15 +61,12 @@
     theta,
     gather,
     place,
-    perm,
     select,
     tsend,
     tmid,
     tturn,
     ttag,
     wsend,
-    wmid,
-    wturn,
     wrecv,
     t_ext,
     k_ext,
@@ -172,7 +169,7 @@
     owner = owner_ref[...]
     to_a = (owner // NPY).astype(F32) * CAP + pos
     to_b = (owner % NPY).astype(F32)
-    dest = to_b * LINES + to_a
+    dest = owner.astype(F32) * CAP + pos
     place[...] = (iota((SLOTS, YB), 0).astype(F32) == dest).astype(F32).astype(BF)
     name = row_ref[...].astype(F32) + 1.0
     named = jnp.where(
@@ -218,17 +215,6 @@
         ).start()
 
     along_y(tsend, tmid, 8, 2)
-    r_to = iota((SLOTS, SLOTS), 0)
-    perm[...] = (
-        (
-            iota((SLOTS, SLOTS), 1)
-            == ((r_to % (NPY * CAP)) // CAP) * LINES
-            + (r_to // (NPY * CAP)) * CAP
-            + r_to % CAP
-        )
-        .astype(F32)
-        .astype(BF)
-    )
     tcol = jnp.broadcast_to(tile_ref[...].astype(F32), (YB, YB)).T
     for n in range(NZ * XB // YB):
         gather[:, n * YB : (n + 1) * YB] = (
@@ -474,31 +460,50 @@
     got_half(3)
     pass_y(3)
     pass_y(1)
-
+    got_x(2)
+    pass_x(2)
     wait_bytes(theta, r4.at[3])
     keep_theta = pltpu.make_async_copy(theta, out.at[3], copy_sem)
     keep_theta.start()
     lines = theta[...].reshape(NZ * XB, YB)
     flux = jnp.dot(gather[...], lines, preferred_element_type=F32).astype(BF)
-    wsend[...] = jnp.dot(place[...], flux, preferred_element_type=F32).astype(BF)
-    along_y(wsend, wmid, LINES, 0)
-
-    got_x(2)
-    pass_x(2)
-    wait_bytes(wmid, rw.at[0])
-    wturn[...] = jnp.dot(perm[...], wmid[...], preferred_element_type=F32).astype(BF)
-    along_x(wturn, wrecv, NPY * CAP, 1)
+    wsend[...] = (
+        jnp.dot(place[...], flux, preferred_element_type=F32)
+        .reshape(DEV, CAP, YB)
+        .astype(BF)
+    )
+
+    def send_wall(to_a, to_b):
+        pltpu.make_async_remote_copy(
+            src_ref=wsend.at[to_a * NPY + to_b],
+            dst_ref=wrecv.at[me],
+            send_sem=sw.at[0],
+            recv_sem=rw.at[0],
+            device_id=(to_a, to_b),
+            device_id_type=MESH,
+        ).start()
+
+    near = [(b + n) % NPY for n in range(NPY)]
+
+    @pl.loop(1, NPX)
+    def _(d):
+        for to_b in near:
+            send_wall((a + d) % NPX, to_b)
+
+    for to_b in near[1:]:
+        send_wall(a, to_b)
+    pltpu.make_async_copy(wsend.at[me], wrecv.at[me], rw.at[0]).start()
 
     got_half(0)
     pass_y(0)
+    wait_bytes(wrecv, rw.at[0])
+    arrived = wrecv[...].astype(F32).reshape(SLOTS, YB).astype(BF)
+    source = jnp.dot(select[...], arrived, preferred_element_type=F32)
+    s_ext[HALO : HALO + XB, YB : 2 * YB] = source * (source_gain * wall_gain)
+
+    halo(s_ext, HALO, s_ext, sh.at[2], rh.at[2])
     got_half(2)
     pass_y(2)
-
-    wait_bytes(wrecv, rw.at[1])
-    source = jnp.dot(select[...], wrecv[...], preferred_element_type=F32)
-    s_ext[HALO : HALO + XB, YB : 2 * YB] = source * (source_gain * wall_gain)
-
-    halo(s_ext, HALO, s_ext, sh.at[2], rh.at[2])
     halo_wait(s_ext, sh.at[2], rh.at[2], False)
 
     heat = jnp.where(inside, s_ext[...], 0.0)
@@ -528,8 +533,7 @@
             wait_bytes(half.at[f], s2.at[f])
 
         wait_bytes(ysend.at[f, pl.ds(0, NPY - 1)], s4.at[f])
-    wait_bytes(wsend.at[pl.ds(0, (NPY - 1) * LINES)], sw.at[0])
-    wait_bytes(wturn.at[pl.ds(0, (NPX - 1) * NPY * CAP)], sw.at[1])
+    wait_bytes(wsend.at[pl.ds(0, DEV - 1)], sw.at[0])
     wait_bytes(tsend.at[pl.ds(0, (NPY - 1) * 8)], sw.at[2])
     wait_bytes(tturn.at[pl.ds(0, (NPX - 1) * 8)], sw.at[3])
 
@@ -592,16 +596,13 @@
             pltpu.VMEM((NZ, XB, YB), BF),
             pltpu.VMEM((YB, NZ * XB), BF),
             pltpu.VMEM((SLOTS, YB), BF),
-            pltpu.VMEM((SLOTS, SLOTS), BF),
             pltpu.VMEM((XB, SLOTS), BF),
             pltpu.VMEM((NPY * 8, YB), BF),
             pltpu.VMEM((NPY * 8, YB), BF),
             pltpu.VMEM((NPX * 8, YB), BF),
             pltpu.VMEM((NPX * 8, YB), BF),
-            pltpu.VMEM((SLOTS, YB), BF),
-            pltpu.VMEM((SLOTS, YB), BF),
-            pltpu.VMEM((SLOTS, YB), BF),
-            pltpu.VMEM((SLOTS, YB), BF),
+            pltpu.VMEM((DEV, CAP, YB), BF),
+            pltpu.VMEM((DEV, CAP, YB), BF),
             pltpu.VMEM((ROWS, COLS), F32),
             pltpu.VMEM((ROWS, COLS), F32),
             pltpu.VMEM((ROWS, COLS), F32),

time: 57.1 us -> 54.3 us (0.951)
  Pallas kernels: 56.3 us -> 53.6 us
    pallas_call x1, Pallas kernels: 54.3 us -> 51.6 us  [on_device(): pl.pallas_call(kernel, out_shape=(jax.ShapeDtypeStruct(fields.shape, BF),...]
where the time goes in v3:
time: 54.3 us; the launch traced here: 54.2 us
  Pallas kernels  53.6 us (99%)
  between operations  0.64 us (1%)
    pallas_call x1, Pallas kernels, on_device(): pl.pallas_call(kernel, out_shape=(jax.ShapeDtypeStruct(fields.shape, BF),...  51.6 us
    pallas_call x1, Pallas kernels, on_device(): pl.pallas_call(finish, out_shape=(jax.ShapeDtypeStruct(fields.shape, BF),...  2 us

profile of v3, /device:TPU:1, one launch (start us, length us, event | category | flops | bytes accessed | tf_op | source)
XLA Modules:
  0.0 54.2 jit_solution(7794475875349811373)
XLA Ops:
  0.6 51.6 %substep.1 = (bf16[4,16,64,128]{3,2,1,0:T(8,128)(2,1)}, f32[64,128]{1,0:T(8,128)}) custom-call(bf16[4,16,64,128]{3,2,1,0:T(8,128)(2,1)} %fields.1, bf16[3,1024,1024]{2,1,0:T(8,128)(2,1)} %xop_hbm.1, bf16[3,1024,1024]{2,1,0:T(8,128)(2,1)} %yop_hbm.1, f32[4]{0:T(128)} %visc_hbm.1, s32[1,128]{1,0:T(1,128)} %bitcast.3, s32[1,128]{1,0:T(1,128)} %bitcast.4, ...), custom_call_target="tpu_custom_call" | custom-call | tf_op jit(solution)/shard_map/substep/pallas_call | solution.py:575
  52.2 2.0 %finish.1 = (bf16[4,16,64,128]{3,2,1,0:T(8,128)(2,1)}, f32[64,128]{1,0:T(8,128)}) custom-call(bf16[4,16,64,128]{3,2,1,0:T(8,128)(2,1)} %get-tuple-element.4.fields_in, f32[64,128]{1,0:T(8,128)} %get-tuple-element.5.solid_in), custom_call_target="tpu_custom_call" | custom-call | tf_op jit(solution)/shard_map/finish/pallas_call | solution.py:639

commit v4 on v3

--- a/solution.py
+++ b/solution.py
@@ -54,6 +54,8 @@
     xop,
     yop,
     yopt,
+    xsum,
+    ysum,
     xrows,
     half,
     yrows,
@@ -289,12 +291,16 @@
         rr = pl.ds(pl.multiple_of(tile * TILE, TILE), TILE)
         q = xrows[f]
         r0 = jnp.dot(xop[0, rr, :], q, preferred_element_type=F32)
-        r1_ = jnp.dot(xop[1, rr, :], q, preferred_element_type=F32)
-        r2_ = jnp.dot(xop[2, rr, :], q, preferred_element_type=F32)
         speed = xrows[0, rr, :].astype(F32)
-        half[f, rr, :] = (
-            r2_ + time_step * (-speed * r0 + visc[f] * r1_)
-        ).astype(BF)
+        if f in (1, 3):
+            rest = jnp.dot(xsum[f // 2, rr, :], q, preferred_element_type=F32)
+            half[f, rr, :] = (rest - time_step * (speed * r0)).astype(BF)
+        else:
+            r1_ = jnp.dot(xop[1, rr, :], q, preferred_element_type=F32)
+            r2_ = jnp.dot(xop[2, rr, :], q, preferred_element_type=F32)
+            half[f, rr, :] = (
+                r2_ + time_step * (-speed * r0 + visc[f] * r1_)
+            ).astype(BF)
 
     tiles = NPX * XB // TILE
 
@@ -405,6 +411,15 @@
     along_x(tturn, ttag, 8, 3)
 
     xload.wait()
+
+    @pl.loop(0, NPX * XB // 32)
+    def _(n):
+        rr = pl.ds(pl.multiple_of(n * 32, 32), 32)
+        second = time_step * xop[1, rr, :].astype(F32)
+        smooth = xop[2, rr, :].astype(F32)
+        xsum[0, rr, :] = (smooth + visc[1] * second).astype(BF)
+        xsum[1, rr, :] = (smooth + visc[3] * second).astype(BF)
+
     got_x(0)
     got_x(1)
     pass_x(1)
@@ -589,6 +604,8 @@
             pltpu.VMEM((3, NPX * XB, NPX * XB), BF),
             pltpu.VMEM((3, NPY * YB, NPY * YB), BF),
             pltpu.VMEM((3, NPY * YB, NPY * YB), BF),
+            pltpu.VMEM((2, NPX * XB, NPX * XB), BF),
+            pltpu.VMEM((NPY * YB, NPY * YB), BF),
             pltpu.VMEM((F, NPX * XB, YB), BF),
             pltpu.VMEM((F, NPX * XB, YB), BF),
             pltpu.VMEM((F, NPY, 2 * XB, YB), BF),

time: 54.3 us -> 54.1 us (level); the launches traced: 54.2 us -> 53.4 us
  Pallas kernels: 53.6 us -> 52.7 us
    pallas_call x1, Pallas kernels: 51.6 us -> 50.7 us  [on_device(): pl.pallas_call(kernel, out_shape=(jax.ShapeDtypeStruct(fields.shape, BF),...]
where the time goes in v4:
time: 54.1 us; the launch traced here: 53.4 us
  Pallas kernels  52.7 us (97%)
  between operations  0.64 us (1%)
    pallas_call x1, Pallas kernels, on_device(): pl.pallas_call(kernel, out_shape=(jax.ShapeDtypeStruct(fields.shape, BF),...  50.7 us
    pallas_call x1, Pallas kernels, on_device(): pl.pallas_call(finish, out_shape=(jax.ShapeDtypeStruct(fields.shape, BF),...  2 us

profile of v4, /device:TPU:1, one launch (start us, length us, event | category | flops | bytes accessed | tf_op | source)
XLA Modules:
  0.0 53.4 jit_solution(10830292116891458037)
XLA Ops:
  0.6 50.7 %substep.1 = (bf16[4,16,64,128]{3,2,1,0:T(8,128)(2,1)}, f32[64,128]{1,0:T(8,128)}) custom-call(bf16[4,16,64,128]{3,2,1,0:T(8,128)(2,1)} %fields.1, bf16[3,1024,1024]{2,1,0:T(8,128)(2,1)} %xop_hbm.1, bf16[3,1024,1024]{2,1,0:T(8,128)(2,1)} %yop_hbm.1, f32[4]{0:T(128)} %visc_hbm.1, s32[1,128]{1,0:T(1,128)} %bitcast.3, s32[1,128]{1,0:T(1,128)} %bitcast.4, ...), custom_call_target="tpu_custom_call" | custom-call | tf_op jit(solution)/shard_map/substep/pallas_call | solution.py:590
  51.4 2.0 %finish.1 = (bf16[4,16,64,128]{3,2,1,0:T(8,128)(2,1)}, f32[64,128]{1,0:T(8,128)}) custom-call(bf16[4,16,64,128]{3,2,1,0:T(8,128)(2,1)} %get-tuple-element.4.fields_in, f32[64,128]{1,0:T(8,128)} %get-tuple-element.5.solid_in), custom_call_target="tpu_custom_call" | custom-call | tf_op jit(solution)/shard_map/finish/pallas_call | solution.py:656

commit v5 on v4

--- a/solution.py
+++ b/solution.py
@@ -19,6 +19,7 @@
 XB = 64
 YB = 128
 CAP = 4
+PIECES = 16
 LINES = NPX * CAP
 SLOTS = DEV * CAP
 HALO = 8
@@ -554,9 +555,13 @@
 
 
 def finish(fields_in, solid_in, fields_out, solid_out, held, solid, sem_in, sem_out):
-    pieces = [
-        (fields_in.at[f], held.at[f], fields_out.at[f]) for f in range(F)
-    ] + [(solid_in, solid, solid_out)]
+    part = NZ * F // PIECES
+    pieces = [(solid_in, solid, solid_out)]
+    for n in range(PIECES):
+        f, layers = n * part // NZ, pl.ds(n * part % NZ, part)
+        pieces.append(
+            (fields_in.at[f, layers], held.at[f, layers], fields_out.at[f, layers])
+        )
     loads = [
         pltpu.make_async_copy(src, mid, sem_in.at[n])
         for n, (src, mid, _) in enumerate(pieces)
@@ -664,8 +669,8 @@
         scratch_shapes=[
             pltpu.VMEM((F, NZ, XB, YB), BF),
             pltpu.VMEM((XB, YB), F32),
-            dma((F + 1,)),
-            dma((F + 1,)),
+            dma((PIECES + 1,)),
+            dma((PIECES + 1,)),
         ],
         compiler_params=pltpu.CompilerParams(vmem_limit_bytes=67_043_328),
         name="finish",

time: 54.1 us -> 54.3 us (level)
  no operation moved by 1% of the time
where the time goes in v5:
time: 54.3 us; the launch traced here: 53.5 us
  Pallas kernels  52.9 us (97%)
  between operations  0.64 us (1%)
    pallas_call x1, Pallas kernels, on_device(): pl.pallas_call(kernel, out_shape=(jax.ShapeDtypeStruct(fields.shape, BF),...  50.7 us
    pallas_call x1, Pallas kernels, on_device(): pl.pallas_call(finish, out_shape=(jax.ShapeDtypeStruct(fields.shape, BF),...  2.19 us

profile of v5, /device:TPU:1, one launch (start us, length us, event | category | flops | bytes accessed | tf_op | source)
XLA Modules:
  0.0 53.5 jit_solution(13190085181431902220)
XLA Ops:
  0.6 50.7 %substep.1 = (bf16[4,16,64,128]{3,2,1,0:T(8,128)(2,1)}, f32[64,128]{1,0:T(8,128)}) custom-call(bf16[4,16,64,128]{3,2,1,0:T(8,128)(2,1)} %fields.1, bf16[3,1024,1024]{2,1,0:T(8,128)(2,1)} %xop_hbm.1, bf16[3,1024,1024]{2,1,0:T(8,128)(2,1)} %yop_hbm.1, f32[4]{0:T(128)} %visc_hbm.1, s32[1,128]{1,0:T(1,128)} %bitcast.3, s32[1,128]{1,0:T(1,128)} %bitcast.4, ...), custom_call_target="tpu_custom_call" | custom-call | tf_op jit(solution)/shard_map/substep/pallas_call | solution.py:595
  51.4 2.2 %finish.1 = (bf16[4,16,64,128]{3,2,1,0:T(8,128)(2,1)}, f32[64,128]{1,0:T(8,128)}) custom-call(bf16[4,16,64,128]{3,2,1,0:T(8,128)(2,1)} %get-tuple-element.4.fields_in, f32[64,128]{1,0:T(8,128)} %get-tuple-element.5.solid_in), custom_call_target="tpu_custom_call" | custom-call | tf_op jit(solution)/shard_map/finish/pallas_call | solution.py:661

commit v6 on v4

--- a/solution.py
+++ b/solution.py
@@ -292,8 +292,8 @@
         q = xrows[f]
         r0 = jnp.dot(xop[0, rr, :], q, preferred_element_type=F32)
         speed = xrows[0, rr, :].astype(F32)
-        if f in (1, 3):
-            rest = jnp.dot(xsum[f // 2, rr, :], q, preferred_element_type=F32)
+        if f > 0:
+            rest = jnp.dot(xsum[f - 1, rr, :], q, preferred_element_type=F32)
             half[f, rr, :] = (rest - time_step * (speed * r0)).astype(BF)
         else:
             r1_ = jnp.dot(xop[1, rr, :], q, preferred_element_type=F32)
@@ -418,7 +418,8 @@
         second = time_step * xop[1, rr, :].astype(F32)
         smooth = xop[2, rr, :].astype(F32)
         xsum[0, rr, :] = (smooth + visc[1] * second).astype(BF)
-        xsum[1, rr, :] = (smooth + visc[3] * second).astype(BF)
+        xsum[1, rr, :] = (smooth + visc[2] * second).astype(BF)
+        xsum[2, rr, :] = (smooth + visc[3] * second).astype(BF)
 
     got_x(0)
     got_x(1)
@@ -604,7 +605,7 @@
             pltpu.VMEM((3, NPX * XB, NPX * XB), BF),
             pltpu.VMEM((3, NPY * YB, NPY * YB), BF),
             pltpu.VMEM((3, NPY * YB, NPY * YB), BF),
-            pltpu.VMEM((2, NPX * XB, NPX * XB), BF),
+            pltpu.VMEM((3, NPX * XB, NPX * XB), BF),
             pltpu.VMEM((NPY * YB, NPY * YB), BF),
             pltpu.VMEM((F, NPX * XB, YB), BF),
             pltpu.VMEM((F, NPX * XB, YB), BF),

time: 54.1 us -> 55.1 us (1.018); the launches traced: 53.4 us -> 55 us
  Pallas kernels: 52.7 us -> 54.4 us
    pallas_call x1, Pallas kernels: 50.7 us -> 52.4 us  [on_device(): pl.pallas_call(kernel, out_shape=(jax.ShapeDtypeStruct(fields.shape, BF),...]
where the time goes in v6:
time: 55.1 us; the launch traced here: 55 us
  Pallas kernels  54.4 us (99%)
  between operations  0.64 us (1%)
    pallas_call x1, Pallas kernels, on_device(): pl.pallas_call(kernel, out_shape=(jax.ShapeDtypeStruct(fields.shape, BF),...  52.4 us
    pallas_call x1, Pallas kernels, on_device(): pl.pallas_call(finish, out_shape=(jax.ShapeDtypeStruct(fields.shape, BF),...  2 us

profile of v6, /device:TPU:1, one launch (start us, length us, event | category | flops | bytes accessed | tf_op | source)
XLA Modules:
  0.0 55.0 jit_solution(10586211223570789213)
XLA Ops:
  0.6 52.4 %substep.1 = (bf16[4,16,64,128]{3,2,1,0:T(8,128)(2,1)}, f32[64,128]{1,0:T(8,128)}) custom-call(bf16[4,16,64,128]{3,2,1,0:T(8,128)(2,1)} %fields.1, bf16[3,1024,1024]{2,1,0:T(8,128)(2,1)} %xop_hbm.1, bf16[3,1024,1024]{2,1,0:T(8,128)(2,1)} %yop_hbm.1, f32[4]{0:T(128)} %visc_hbm.1, s32[1,128]{1,0:T(1,128)} %bitcast.3, s32[1,128]{1,0:T(1,128)} %bitcast.4, ...), custom_call_target="tpu_custom_call" | custom-call | tf_op jit(solution)/shard_map/substep/pallas_call | solution.py:591
  53.0 2.0 %finish.1 = (bf16[4,16,64,128]{3,2,1,0:T(8,128)(2,1)}, f32[64,128]{1,0:T(8,128)}) custom-call(bf16[4,16,64,128]{3,2,1,0:T(8,128)(2,1)} %get-tuple-element.4.fields_in, f32[64,128]{1,0:T(8,128)} %get-tuple-element.5.solid_in), custom_call_target="tpu_custom_call" | custom-call | tf_op jit(solution)/shard_map/finish/pallas_call | solution.py:657
